TPU v7x, 256 devices: a whole 4x4x8 slice. The times are simulated.
256 devices in a mesh: narrow: 8 (over y, core), wide: 32 (over z, x).
Axes of the slice: x: 4, y: 4, z: 8, core: 2. Of those that a mesh axis runs over, the one named last changes fastest.
Arguments:
- queries: bfloat16 [262144, 128], P(('wide', 'narrow')), may hold values from -0.5 to 0.5
- keys: bfloat16 [262144, 128], P(('wide', 'narrow')), may hold values from -6 to 6
- values: bfloat16 [262144, 1024], P(('wide', 'narrow')), may hold values from -6 to 6
- log_decay: float32 [8, 262144], P(None, ('wide', 'narrow')), may hold values from -1 to 0
- level_weight: float32 [11, 8, 262144], P(None, None, ('wide', 'narrow')), may hold values from 0 to 2
- norm_gain: float32 [1024], replicated, may hold values from 0.5 to 1.5
Outputs:
- layer_output: bfloat16 [262144, 1024], P(('wide', 'narrow'))
All inputs are finite; a program needn't handle non-finite values.
Results may differ from a plain program's by a relative error of at most 0.005.
Values sent between devices are 32-bit elements; how exact they have to be, the bound alone decides.
A program may use at most 128 MiB of HBM per device.

v0:
```python
import jax
import jax.numpy as jnp
import numpy as np
from jax import lax
from jax.sharding import PartitionSpec as P

SPAN = 256


def partner(value, axis, distance):
    mask = 2**distance
    pairs = [(source, source ^ mask) for source in range(lax.axis_size(axis))]
    return lax.ppermute(value, axis, pairs)


def doubling(state, total, trade, bit_count, position):
    prefix = jnp.zeros_like(total)
    found = []
    for bit in range(bit_count):
        other_state, other_total = trade(state, total, bit)
        upper = jnp.bitwise_and(jnp.right_shift(position, bit), 1) == 1
        found.append(jnp.where(upper, other_state * jnp.exp(prefix)[:, None, None], 0.0))
        prefix = jnp.where(upper, prefix + other_total, prefix)
        state = jnp.where(
            upper,
            other_state * jnp.exp(total)[:, None, None] + state,
            state * jnp.exp(other_total)[:, None, None] + other_state,
        )
        total = total + other_total
    levels_found = jnp.stack(found)
    return (levels_found, state, total, prefix)


def per_device(queries, keys, values, log_decay, level_weight, norm_gain):
    tokens_here, key_width = queries.shape
    heads = log_decay.shape[0]
    head_width = values.shape[1] // heads
    level_count = level_weight.shape[0]
    blocks = tokens_here // SPAN
    local_bits = blocks.bit_length() - 1
    query_blocks = queries.reshape(blocks, SPAN, key_width)
    key_blocks = keys.reshape(blocks, SPAN, key_width)
    value_blocks = values.reshape(blocks, SPAN, heads, head_width)
    decay_blocks = log_decay.reshape(heads, blocks, SPAN).transpose(1, 0, 2)
    within = jnp.cumsum(decay_blocks, axis=2)
    block_totals = within[:, :, -1]
    weights = level_weight.reshape(level_count, heads, blocks, SPAN).transpose(0, 2, 1, 3)
    scores = jnp.einsum(
        "cin,cjn->cij", query_blocks, key_blocks, preferred_element_type=jnp.float32
    )
    positions = jnp.arange(SPAN)
    causal = positions[:, None] >= positions[None, :]
    spread = jnp.where(causal, within[:, :, :, None] - within[:, :, None, :], -1e30)
    mixing = (scores[:, None] * jnp.exp(spread) * weights[0][:, :, :, None]).astype(jnp.bfloat16)
    intra = jnp.einsum("chij,cjhp->chip", mixing, value_blocks, preferred_element_type=jnp.float32)
    decayed_keys = (
        jnp.exp(block_totals[:, :, None] - within)[:, :, :, None]
        * key_blocks[:, None].astype(jnp.float32)
    ).astype(jnp.bfloat16)
    states = jnp.einsum(
        "chjn,cjhp->chnp", decayed_keys, value_blocks, preferred_element_type=jnp.float32
    )
    ends = jnp.cumsum(block_totals, axis=0)
    starts = ends - block_totals
    device_state = jnp.einsum(
        "ch,chnp->hnp", jnp.exp(ends[-1][None, :] - ends), states, precision=lax.Precision.HIGHEST
    )
    device_total = ends[-1]
    narrow_place = lax.axis_index("narrow")
    narrow_bits = lax.axis_size("narrow").bit_length() - 1
    narrow_levels, group_state, group_total, narrow_prefix = doubling(
        device_state,
        device_total,
        lambda state, total, bit: partner((state, total), "narrow", bit),
        narrow_bits,
        narrow_place,
    )
    wide_place = lax.axis_index("wide")
    wide_bits = lax.axis_size("wide").bit_length() - 1
    wide_levels, outer_state, outer_total, wide_prefix = doubling(
        group_state,
        group_total,
        lambda state, total, bit: partner((state, total), "wide", bit),
        wide_bits,
        wide_place,
    )
    inter = jnp.zeros_like(intra)
    members = np.zeros((local_bits, blocks, blocks), np.float32)
    for bit in range(local_bits):
        for target in range(blocks):
            for source in range(blocks):
                if target >> bit & 1 == 1 and source >> bit == target >> bit ^ 1:
                    members[bit, target, source] = 1.0
    later = np.arange(blocks)[:, None] > np.arange(blocks)[None, :]
    later_mask = jnp.asarray(later)[:, :, None]
    fades = jnp.where(
        later_mask, jnp.exp(jnp.where(later_mask, starts[:, None, :] - ends[None, :, :], 0.0)), 0.0
    )
    for bit in range(local_bits):
        factors = jnp.asarray(members[bit])[:, :, None] * fades
        level_here = jnp.einsum(
            "cdh,dhnp->chnp", factors, states, precision=lax.Precision.HIGHEST
        ).astype(jnp.bfloat16)
        projected = jnp.einsum(
            "cin,chnp->chip", query_blocks, level_here, preferred_element_type=jnp.float32
        )
        inter = inter + weights[1 + bit][:, :, :, None] * projected
    device_levels = jnp.concatenate(
        [narrow_levels, wide_levels * jnp.exp(narrow_prefix)[None, :, None, None]], axis=0
    )
    start_fades = jnp.exp(starts)[:, :, None, None]

    def add_level(level, running):
        chosen = lax.dynamic_index_in_dim(device_levels, level, 0, keepdims=False)
        per_block = (start_fades * chosen[None]).astype(jnp.bfloat16)
        projected = jnp.einsum(
            "cin,chnp->chip", query_blocks, per_block, preferred_element_type=jnp.float32
        )
        level_scale = lax.dynamic_index_in_dim(weights, 1 + local_bits + level, 0, keepdims=False)
        return running + level_scale[:, :, :, None] * projected

    inter = lax.fori_loop(0, device_levels.shape[0], add_level, inter)
    mixed = intra + jnp.exp(within)[:, :, :, None] * inter
    square = jnp.mean(mixed * mixed, axis=-1, keepdims=True)
    gain_rows = norm_gain.reshape(heads, head_width)
    normed = mixed * lax.rsqrt(square + 1e-05) * gain_rows[None, :, None, :]
    return (
        normed.transpose(0, 2, 1, 3).reshape(tokens_here, heads * head_width).astype(jnp.bfloat16)
    )


def solution(mesh):
    placed = (
        P(("wide", "narrow"), None),
        P(("wide", "narrow"), None),
        P(("wide", "narrow"), None),
        P(None, ("wide", "narrow")),
        P(None, None, ("wide", "narrow")),
        P(),
    )
    return jax.shard_map(
        per_device,
        mesh=mesh,
        in_specs=placed,
        out_specs=P(("wide", "narrow"), None),
        check_vma=False,
    )
```

profile of v0, /device:TPU:230, one launch (start us, length us, event | category | flops | bytes accessed | tf_op | source)
XLA Modules:
  0.0 215.4 jit_solution(12739499533875339424)
XLA Ops:
  0.0 4.2 %reduce-window.6 = f32[4,8,2,128]{3,1,2,0:T(8,128)S(1)} reduce-window(f32[4,8,2,128]{3,1,2,0:T(8,128)} %bitcast.125, f32[]{:T(128)} %constant.85.clone.1), window={size=1x1x1x128 pad=0_0x0_0x0_0x127_0}, to_apply=%region_0.0 | reduce-window | flops 1040384 | bytes 65540 | tf_op jit(solution)/shard_map/reduce-window
  4.8 3.5 %copy.48 = bf16[128,8,8,128]{3,2,1,0:T(8,128)(2,1)} copy(bf16[128,8,8,128]{3,1,2,0:T(8,128)(2,1)} %bitcast.117) | data formatting | bytes 4194304
  19.4 5.2 %fusion.29 = bf16[4,8,128,128]{3,0,2,1:T(4,128)(2,1)} fusion(f32[4,8,128,128]{3,2,1,0:T(8,128)S(1)} %get-tuple-element.217, f32[4,8]{0,1:T(8,128)S(1)} %copy.31, f32[4,8]{0,1:T(8,128)S(1)} %copy.30, f32[4,4]{1,0:T(4,128)S(1)} %copy-done.13, pred[4,4]{1,0:T(4,128)(4,1)S(1)} %copy-done.14), kind=kOutput, calls=%fused_computation.36 | convolution fusion | flops 25690624 | bytes 3146064 | tf_op jit(solution)/shard_map/cdh,dhnp->chnp/dot_general | solution.py:101
  24.6 4.4 %fusion.26 = bf16[4,8,128,128]{3,0,2,1:T(4,128)(2,1)S(1)} fusion(f32[4,8,128,128]{3,2,1,0:T(8,128)S(1)} %get-tuple-element.217, f32[4,4]{1,0:T(4,128)S(1)} %copy-done.12, f32[4,8]{0,1:T(8,128)S(1)} %copy.31, f32[4,8]{0,1:T(8,128)S(1)} %copy.30, pred[4,4]{1,0:T(4,128)(4,1)S(1)} %copy-done.14), kind=kOutput, calls=%fused_computation.35 | convolution fusion | flops 25690624 | bytes 3146064 | tf_op jit(solution)/shard_map/cdh,dhnp->chnp/dot_general | solution.py:101
  30.9 3.3 %collective-permute-start.4 = (f32[8,128,128]{1,2,0:T(8,128)S(1)}, f32[8,128,128]{1,2,0:T(8,128)}, u32[]{:S(2)}, u32[]{:S(2)}) collective-permute-start(f32[8,128,128]{1,2,0:T(8,128)S(1)} %get-tuple-element.193), channel_id=1, source_target_pairs={{0,128},{32,160},{64,192},{96,224},{128,0},{160,32},{192,64},{224,... | collective-permute-start | bytes 1572872 | tf_op jit(solution)/shard_map/ppermute | solution.py:13
  35.8 8.7 %collective-permute-done.5 = f32[8]{0:T(128)S(1)} collective-permute-done((f32[8]{0:T(128)S(1)}, f32[8]{0:T(128)S(1)}, u32[]{:S(2)}, u32[]{:S(2)}) %collective-permute-start.5) | collective-permute-done | bytes 64 | tf_op jit(solution)/shard_map/ppermute | solution.py:13
  45.9 2.7 %collective-permute-done.7 = f32[8]{0:T(128)S(1)} collective-permute-done((f32[8]{0:T(128)S(1)}, f32[8]{0:T(128)S(1)}, u32[]{:S(2)}, u32[]{:S(2)}) %collective-permute-start.7) | collective-permute-done | bytes 64 | tf_op jit(solution)/shard_map/ppermute | solution.py:13
  58.8 3.0 %collective-permute-done.13 = f32[8]{0:T(128)S(1)} collective-permute-done((f32[8]{0:T(128)S(1)}, f32[8]{0:T(128)S(1)}, u32[]{:S(2)}, u32[]{:S(2)}) %collective-permute-start.13) | collective-permute-done | bytes 64 | tf_op jit(solution)/shard_map/ppermute | solution.py:13
  67.6 6.6 %collective-permute-done.8 = f32[8,128,128]{1,2,0:T(8,128)S(1)} collective-permute-done((f32[8,128,128]{1,2,0:T(8,128)S(1)}, f32[8,128,128]{1,2,0:T(8,128)S(1)}, u32[]{:S(2)}, u32[]{:S(2)}) %collective-permute-start.8) | collective-permute-done | bytes 524320 | tf_op jit(solution)/shard_map/ppermute | solution.py:13
  76.3 2.8 %add_bitcast_fusion = f32[4,8,256,128]{2,3,1,0:T(8,128)} fusion(f32[4,8,128,256]{3,2,1,0:T(8,128)S(1)} %fusion.33, bf16[4,256,128,1]{2,1,3,0:T(8,128)(2,1)S(1)} %bitcast.114, f32[4,8,256]{2,1,0:T(8,128)S(1)} %get-tuple-element.197, f32[4,8,256]{2,1,0:T(8,128)S(1)} %get-tuple-element.198, bf16[4,8,128,128]{3,0,2,1:T(4,128)(2,1)S(1)} %fusion.26), kind=kOutput, calls=%fused_computation.13 | convolution fusion | flops 271581184 | bytes 9764864 | tf_op jit(solution)/shard_map/cin,chnp->chip/dot_general | solution.py:104
  79.2 8.1 %collective-permute-done.10 = f32[8,128,128]{1,2,0:T(8,128)S(1)} collective-permute-done((f32[8,128,128]{1,2,0:T(8,128)S(1)}, f32[8,128,128]{1,2,0:T(8,128)S(1)}, u32[]{:S(2)}, u32[]{:S(2)}) %collective-permute-start.10) | collective-permute-done | bytes 524320 | tf_op jit(solution)/shard_map/ppermute | solution.py:13
  90.7 36.7 %collective-permute-done.12 = f32[8,128,128]{1,2,0:T(8,128)S(1)} collective-permute-done((f32[8,128,128]{1,2,0:T(8,128)S(1)}, f32[8,128,128]{1,2,0:T(8,128)S(1)}, u32[]{:S(2)}, u32[]{:S(2)}) %collective-permute-start.12) | collective-permute-done | bytes 524320 | tf_op jit(solution)/shard_map/ppermute | solution.py:13
  129.3 15.0 %collective-permute-done.14 = f32[8,128,128]{1,2,0:T(8,128)S(1)} collective-permute-done((f32[8,128,128]{1,2,0:T(8,128)S(1)}, f32[8,128,128]{1,2,0:T(8,128)S(1)}, u32[]{:S(2)}, u32[]{:S(2)}) %collective-permute-start.14) | collective-permute-done | bytes 524320 | tf_op jit(solution)/shard_map/ppermute | solution.py:13
  147.7 54.9 %while.15 = (s32[]{:T(128)}, f32[4,8,256,128]{2,3,1,0:T(8,128)}, f32[11,4,8,256]{3,2,1,0:T(8,128)}, f32[4,8,1,1]{1,0,3,2:T(4,128)S(1)}, f32[8,8,128,128]{2,3,1,0...) while((s32[]{:T(128)}, f32[4,8,256,128]{2,3,1,0:T(8,128)}, ...), condition=%wide.region_4.5_spmd, body=%wide.region_3.4_spmd.sunk | while | flops 271581184 | bytes 10322211 | solution.py:122
  149.8 5.0 %bitcast_add_fusion.2 = f32[4,8,256,128]{2,3,1,0:T(8,128)} fusion(f32[4,8,256,128]{2,3,1,0:T(8,128)} %get-tuple-element.268, f32[4,8,256]{2,1,0:T(8,128)S(1)} %dynamic-slice_bitcast_fusion.4, f32[8,128,128]{1,2,0:T(8,128)S(1)} %dynamic-slice_bitcast_fusion.5, f32[4,8]{1,0:T(4,128)S(1)} %bitcast.124, bf16[4,256,128]{2,1,0:T(8,128)(2,1)S(1)} %get-tuple-element.282), kind=kOutput, calls=%fused_computation.clone.1 | convolution fusion | flops 271581184 | bytes 9207936 | tf_op jit(solution)/shard_map/while/body/eval_jaxpr/cin,chnp->chip/dot_general | solution.py:116
  156.6 5.0 %bitcast_add_fusion.2 = f32[4,8,256,128]{2,3,1,0:T(8,128)} fusion(f32[4,8,256,128]{2,3,1,0:T(8,128)} %get-tuple-element.268, f32[4,8,256]{2,1,0:T(8,128)S(1)} %dynamic-slice_bitcast_fusion.4, f32[8,128,128]{1,2,0:T(8,128)S(1)} %dynamic-slice_bitcast_fusion.5, f32[4,8]{1,0:T(4,128)S(1)} %bitcast.124, bf16[4,256,128]{2,1,0:T(8,128)(2,1)S(1)} %get-tuple-element.282), kind=kOutput, calls=%fused_computation.clone.1 | convolution fusion | flops 271581184 | bytes 9207936 | tf_op jit(solution)/shard_map/while/body/eval_jaxpr/cin,chnp->chip/dot_general | solution.py:116
  163.5 5.0 %bitcast_add_fusion.2 = f32[4,8,256,128]{2,3,1,0:T(8,128)} fusion(f32[4,8,256,128]{2,3,1,0:T(8,128)} %get-tuple-element.268, f32[4,8,256]{2,1,0:T(8,128)S(1)} %dynamic-slice_bitcast_fusion.4, f32[8,128,128]{1,2,0:T(8,128)S(1)} %dynamic-slice_bitcast_fusion.5, f32[4,8]{1,0:T(4,128)S(1)} %bitcast.124, bf16[4,256,128]{2,1,0:T(8,128)(2,1)S(1)} %get-tuple-element.282), kind=kOutput, calls=%fused_computation.clone.1 | convolution fusion | flops 271581184 | bytes 9207936 | tf_op jit(solution)/shard_map/while/body/eval_jaxpr/cin,chnp->chip/dot_general | solution.py:116
  170.3 5.0 %bitcast_add_fusion.2 = f32[4,8,256,128]{2,3,1,0:T(8,128)} fusion(f32[4,8,256,128]{2,3,1,0:T(8,128)} %get-tuple-element.268, f32[4,8,256]{2,1,0:T(8,128)S(1)} %dynamic-slice_bitcast_fusion.4, f32[8,128,128]{1,2,0:T(8,128)S(1)} %dynamic-slice_bitcast_fusion.5, f32[4,8]{1,0:T(4,128)S(1)} %bitcast.124, bf16[4,256,128]{2,1,0:T(8,128)(2,1)S(1)} %get-tuple-element.282), kind=kOutput, calls=%fused_computation.clone.1 | convolution fusion | flops 271581184 | bytes 9207936 | tf_op jit(solution)/shard_map/while/body/eval_jaxpr/cin,chnp->chip/dot_general | solution.py:116
  177.2 5.0 %bitcast_add_fusion.2 = f32[4,8,256,128]{2,3,1,0:T(8,128)} fusion(f32[4,8,256,128]{2,3,1,0:T(8,128)} %get-tuple-element.268, f32[4,8,256]{2,1,0:T(8,128)S(1)} %dynamic-slice_bitcast_fusion.4, f32[8,128,128]{1,2,0:T(8,128)S(1)} %dynamic-slice_bitcast_fusion.5, f32[4,8]{1,0:T(4,128)S(1)} %bitcast.124, bf16[4,256,128]{2,1,0:T(8,128)(2,1)S(1)} %get-tuple-element.282), kind=kOutput, calls=%fused_computation.clone.1 | convolution fusion | flops 271581184 | bytes 9207936 | tf_op jit(solution)/shard_map/while/body/eval_jaxpr/cin,chnp->chip/dot_general | solution.py:116
  184.0 5.0 %bitcast_add_fusion.2 = f32[4,8,256,128]{2,3,1,0:T(8,128)} fusion(f32[4,8,256,128]{2,3,1,0:T(8,128)} %get-tuple-element.268, f32[4,8,256]{2,1,0:T(8,128)S(1)} %dynamic-slice_bitcast_fusion.4, f32[8,128,128]{1,2,0:T(8,128)S(1)} %dynamic-slice_bitcast_fusion.5, f32[4,8]{1,0:T(4,128)S(1)} %bitcast.124, bf16[4,256,128]{2,1,0:T(8,128)(2,1)S(1)} %get-tuple-element.282), kind=kOutput, calls=%fused_computation.clone.1 | convolution fusion | flops 271581184 | bytes 9207936 | tf_op jit(solution)/shard_map/while/body/eval_jaxpr/cin,chnp->chip/dot_general | solution.py:116
  190.8 5.0 %bitcast_add_fusion.2 = f32[4,8,256,128]{2,3,1,0:T(8,128)} fusion(f32[4,8,256,128]{2,3,1,0:T(8,128)} %get-tuple-element.268, f32[4,8,256]{2,1,0:T(8,128)S(1)} %dynamic-slice_bitcast_fusion.4, f32[8,128,128]{1,2,0:T(8,128)S(1)} %dynamic-slice_bitcast_fusion.5, f32[4,8]{1,0:T(4,128)S(1)} %bitcast.124, bf16[4,256,128]{2,1,0:T(8,128)(2,1)S(1)} %get-tuple-element.282), kind=kOutput, calls=%fused_computation.clone.1 | convolution fusion | flops 271581184 | bytes 9207936 | tf_op jit(solution)/shard_map/while/body/eval_jaxpr/cin,chnp->chip/dot_general | solution.py:116
  197.7 5.0 %bitcast_add_fusion.2 = f32[4,8,256,128]{2,3,1,0:T(8,128)} fusion(f32[4,8,256,128]{2,3,1,0:T(8,128)} %get-tuple-element.268, f32[4,8,256]{2,1,0:T(8,128)S(1)} %dynamic-slice_bitcast_fusion.4, f32[8,128,128]{1,2,0:T(8,128)S(1)} %dynamic-slice_bitcast_fusion.5, f32[4,8]{1,0:T(4,128)S(1)} %bitcast.124, bf16[4,256,128]{2,1,0:T(8,128)(2,1)S(1)} %get-tuple-element.282), kind=kOutput, calls=%fused_computation.clone.1 | convolution fusion | flops 271581184 | bytes 9207936 | tf_op jit(solution)/shard_map/while/body/eval_jaxpr/cin,chnp->chip/dot_general | solution.py:116
  202.7 5.7 %multiply_reduce_fusion = (f32[4,8,256]{2,1,0:T(8,128)S(1)}, f32[4,8,256,128]{2,3,1,0:T(8,128)S(1)}) fusion(f32[4,8,256,128]{2,3,1,0:T(8,128)} %get-tuple-element.159, f32[4,8,256]{2,1,0:T(8,128)S(1)} %get-tuple-element.172, bf16[4,256,8,128]{3,2,1,0:T(8,128)(2,1)S(1)} %bitcast.119, f32[4,8,256]{2,1,0:T(8,128)} %get-tuple-element.196, ...), kind=kOutput, calls=%fused_computation.11 | convolution fusion | flops 551542784 | bytes 11730944 | tf_op jit(solution)/shard_map/chij,cjhp->chip/dot_general | solution.py:55
  210.3 3.1 %copy.36 = bf16[4,256,8,128]{3,2,1,0:T(8,128)(2,1)S(1)} copy(bf16[4,256,8,128]{1,3,2,0:T(8,128)(2,1)} %fusion.11) | data formatting | bytes 4194304 | tf_op jit(solution)/shard_map/convert_element_type | solution.py:128
  (114 shorter events, 61.8 us)
Async XLA Ops:
  11.0 13.6 %copy-start.12 = (f32[4,4]{1,0:T(4,128)S(1)}, f32[4,4]{1,0:T(4,128)}, u32[]{:S(2)}) copy-start(f32[4,4]{1,0:T(4,128)} %constant.99.clone) | copy-start | bytes 196
  11.2 5.6 %collective-permute-start = (f32[8,128,128]{1,2,0:T(8,128)S(1)}, f32[8,128,128]{1,2,0:T(8,128)S(1)}, u32[]{:S(2)}, u32[]{:S(2)}) collective-permute-start(f32[8,128,128]{1,2,0:T(8,128)S(1)} %copy.46), channel_id=1, source_target_pairs={{0,32},{32,0},{64,96},{96,64},{128,160},{160,128},{192,224},{224,1... | collective-permute-start | bytes 1572872 | tf_op jit(solution)/shard_map/ppermute | solution.py:13
  11.3 1.9 collective-permute-start.1
  13.3 3.6 %collective-permute-start.3 = (f32[8]{0:T(128)S(1)}, f32[8]{0:T(128)S(1)}, u32[]{:S(2)}, u32[]{:S(2)}) collective-permute-start(f32[8]{0:T(128)S(1)} %get-tuple-element.189), channel_id=1, source_target_pairs={{0,64},{32,96},{64,0},{96,32},{128,192},{160,224},{192,128},{224,1... | collective-permute-start | bytes 104 | tf_op jit(solution)/shard_map/ppermute | solution.py:13
  17.8 12.8 %collective-permute-start.2 = (f32[8,128,128]{1,2,0:T(8,128)S(1)}, f32[8,128,128]{1,2,0:T(8,128)S(1)}, u32[]{:S(2)}, u32[]{:S(2)}) collective-permute-start(f32[8,128,128]{1,2,0:T(8,128)S(1)} %get-tuple-element.191), channel_id=1, source_target_pairs={{0,64},{32,96},{64,0},{96,32},{128,192},{160,224},{192,128},{224,1... | collective-permute-start | bytes 1572872 | tf_op jit(solution)/shard_map/ppermute | solution.py:13
  19.4 14.7 %copy-start = (bf16[1024,128]{1,0:T(8,128)(2,1)S(1)}, bf16[1024,128]{1,0:T(8,128)(2,1)}, u32[]{:S(2)}) copy-start(bf16[1024,128]{1,0:T(8,128)(2,1)} %param.11) | copy-start | bytes 786436
  19.4 14.7 %copy-start.10 = (bf16[1024,128]{1,0:T(8,128)(2,1)S(1)}, bf16[1024,128]{1,0:T(8,128)(2,1)}, u32[]{:S(2)}) copy-start(bf16[1024,128]{1,0:T(8,128)(2,1)} %param.12) | copy-start | bytes 786436
  29.0 37.8 %copy-start.1 = (bf16[4,8,128,128]{3,0,2,1:T(4,128)(2,1)S(1)}, bf16[4,8,128,128]{3,0,2,1:T(4,128)(2,1)}, u32[]{:S(2)}) copy-start(bf16[4,8,128,128]{3,0,2,1:T(4,128)(2,1)} %fusion.29) | copy-start | bytes 3145732
  30.8 19.3 %copy-start.2 = (f32[8,128,128]{1,2,0:T(8,128)}, f32[8,128,128]{1,2,0:T(8,128)S(1)}, u32[]{:S(2)}) copy-start(f32[8,128,128]{1,2,0:T(8,128)S(1)} %get-tuple-element.193) | copy-start | bytes 1572868
  30.9 19.2 %collective-permute-start.4 = (f32[8,128,128]{1,2,0:T(8,128)S(1)}, f32[8,128,128]{1,2,0:T(8,128)}, u32[]{:S(2)}, u32[]{:S(2)}) collective-permute-start(f32[8,128,128]{1,2,0:T(8,128)S(1)} %get-tuple-element.193), channel_id=1, source_target_pairs={{0,128},{32,160},{64,192},{96,224},{128,0},{160,32},{192,64},{224,... | collective-permute-start | bytes 1572872 | tf_op jit(solution)/shard_map/ppermute | solution.py:13
  35.5 9.0 %collective-permute-start.5 = (f32[8]{0:T(128)S(1)}, f32[8]{0:T(128)S(1)}, u32[]{:S(2)}, u32[]{:S(2)}) collective-permute-start(f32[8]{0:T(128)S(1)} %get-tuple-element.204), channel_id=1, source_target_pairs={{0,128},{32,160},{64,192},{96,224},{128,0},{160,32},{192,64},{224,... | collective-permute-start | bytes 104 | tf_op jit(solution)/shard_map/ppermute | solution.py:13
  45.1 3.6 %collective-permute-start.7 = (f32[8]{0:T(128)S(1)}, f32[8]{0:T(128)S(1)}, u32[]{:S(2)}, u32[]{:S(2)}) collective-permute-start(f32[8]{0:T(128)S(1)} %get-tuple-element.185), channel_id=1, source_target_pairs={{0,1},{1,0},{2,3},{3,2},{4,5},{5,4},{6,7},{7,6},{8,9},{9,8},{10,11... | collective-permute-start | bytes 104 | tf_op jit(solution)/shard_map/ppermute | solution.py:13
  48.7 5.1 %collective-permute-start.9 = (f32[8]{0:T(128)S(1)}, f32[8]{0:T(128)S(1)}, u32[]{:S(2)}, u32[]{:S(2)}) collective-permute-start(f32[8]{0:T(128)S(1)} %get-tuple-element.183), channel_id=1, source_target_pairs={{0,2},{1,3},{2,0},{3,1},{4,6},{5,7},{6,4},{7,5},{8,10},{9,11},{10,... | collective-permute-start | bytes 104 | tf_op jit(solution)/shard_map/ppermute | solution.py:13
  51.5 11.2 %collective-permute-start.6 = (f32[8,128,128]{1,2,0:T(8,128)S(1)}, f32[8,128,128]{1,2,0:T(8,128)S(1)}, u32[]{:S(2)}, u32[]{:S(2)}) collective-permute-start(f32[8,128,128]{1,2,0:T(8,128)S(1)} %get-tuple-element.195), channel_id=1, source_target_pairs={{0,1},{1,0},{2,3},{3,2},{4,5},{5,4},{6,7},{7,6},{8,9},{9,8},{10,11... | collective-permute-start | bytes 1572872 | tf_op jit(solution)/shard_map/ppermute | solution.py:13
  53.8 3.6 %collective-permute-start.11 = (f32[8]{0:T(128)S(1)}, f32[8]{0:T(128)S(1)}, u32[]{:S(2)}, u32[]{:S(2)}) collective-permute-start(f32[8]{0:T(128)S(1)} %get-tuple-element.181), channel_id=1, source_target_pairs={{0,4},{1,5},{2,6},{3,7},{4,0},{5,1},{6,2},{7,3},{8,12},{9,13},{10,... | collective-permute-start | bytes 104 | tf_op jit(solution)/shard_map/ppermute | solution.py:13
  57.4 4.5 %collective-permute-start.13 = (f32[8]{0:T(128)S(1)}, f32[8]{0:T(128)S(1)}, u32[]{:S(2)}, u32[]{:S(2)}) collective-permute-start(f32[8]{0:T(128)S(1)} %get-tuple-element.179), channel_id=1, source_target_pairs={{0,8},{1,9},{2,10},{3,11},{4,12},{5,13},{6,14},{7,15},{8,0},{9,1},... | collective-permute-start | bytes 104 | tf_op jit(solution)/shard_map/ppermute | solution.py:13
  62.9 11.4 %collective-permute-start.8 = (f32[8,128,128]{1,2,0:T(8,128)S(1)}, f32[8,128,128]{1,2,0:T(8,128)S(1)}, u32[]{:S(2)}, u32[]{:S(2)}) collective-permute-start(f32[8,128,128]{1,2,0:T(8,128)S(1)} %add_select_fusion.3), channel_id=1, source_target_pairs={{0,2},{1,3},{2,0},{3,1},{4,6},{5,7},{6,4},{7,5},{8,10},{9,11},{10,... | collective-permute-start | bytes 1572872 | tf_op jit(solution)/shard_map/ppermute | solution.py:13
  75.2 12.0 %collective-permute-start.10 = (f32[8,128,128]{1,2,0:T(8,128)S(1)}, f32[8,128,128]{1,2,0:T(8,128)S(1)}, u32[]{:S(2)}, u32[]{:S(2)}) collective-permute-start(f32[8,128,128]{1,2,0:T(8,128)S(1)} %add_select_fusion.2), channel_id=1, source_target_pairs={{0,4},{1,5},{2,6},{3,7},{4,0},{5,1},{6,2},{7,3},{8,12},{9,13},{10,... | collective-permute-start | bytes 1572872 | tf_op jit(solution)/shard_map/ppermute | solution.py:13
  79.2 49.2 %copy-start.4 = (f32[8,128,128]{1,2,0:T(8,128)S(1)}, f32[8,128,128]{1,2,0:T(8,128)}, u32[]{:S(2)}) copy-start(f32[8,128,128]{1,2,0:T(8,128)} %copy-done.3) | copy-start | bytes 1572868
  87.4 40.0 %collective-permute-start.12 = (f32[8,128,128]{1,2,0:T(8,128)S(1)}, f32[8,128,128]{1,2,0:T(8,128)S(1)}, u32[]{:S(2)}, u32[]{:S(2)}) collective-permute-start(f32[8,128,128]{1,2,0:T(8,128)S(1)} %add_select_fusion.1), channel_id=1, source_target_pairs={{0,8},{1,9},{2,10},{3,11},{4,12},{5,13},{6,14},{7,15},{8,0},{9,1},... | collective-permute-start | bytes 1572872 | tf_op jit(solution)/shard_map/ppermute | solution.py:13
  128.2 16.1 %collective-permute-start.14 = (f32[8,128,128]{1,2,0:T(8,128)S(1)}, f32[8,128,128]{1,2,0:T(8,128)S(1)}, u32[]{:S(2)}, u32[]{:S(2)}) collective-permute-start(f32[8,128,128]{1,2,0:T(8,128)S(1)} %add_select_fusion), channel_id=1, source_target_pairs={{0,16},{1,17},{2,18},{3,19},{4,20},{5,21},{6,22},{7,23},{8,24},{9,... | collective-permute-start | bytes 1572872 | tf_op jit(solution)/shard_map/ppermute | solution.py:13
  129.0 16.4 %copy-start.7 = (f32[1,8,128,128]{2,3,1,0:T(8,128)S(1)}, f32[1,8,128,128]{2,3,1,0:T(8,128)}, u32[]{:S(2)}) copy-start(f32[1,8,128,128]{2,3,1,0:T(8,128)} %get-tuple-element.190) | copy-start | bytes 1572868
  147.7 55.0 %copy-start.6 = (bf16[128,8,8,128]{3,2,1,0:T(8,128)(2,1)S(1)}, bf16[128,8,8,128]{3,2,1,0:T(8,128)(2,1)}, u32[]{:S(2)}) copy-start(bf16[128,8,8,128]{3,2,1,0:T(8,128)(2,1)} %copy.48) | copy-start | bytes 6291460
  147.7 55.0 %copy-start.8 = (f32[4,256,256]{2,1,0:T(8,128)S(1)}, f32[4,256,256]{2,1,0:T(8,128)}, u32[]{:S(2)}) copy-start(f32[4,256,256]{2,1,0:T(8,128)} %fusion.71) | copy-start | bytes 3145732
  (6 other events, 40.9 us)
where the time goes:
time: 218 us; the launch traced here: 215 us
  waiting for transfers between devices  90.5 us (42%)
  matrix products  62.8 us (29%)
  local copies, waits for them, and re-layouts  26.6 us (12%)
  starting transfers between devices  17.6 us (8%)
  other arithmetic  17.4 us (8%)
    ppermute x15, waiting for transfers between devices, partner(): return lax.ppermute(value, axis, pairs)  90.5 us
    dot_general x8, matrix products, add_level(): jnp.einsum('cin,chnp->chip', query_blocks, per_block, preferred_element_t...  40 us
    ppermute x15, starting transfers between devices, partner(): return lax.ppermute(value, axis, pairs)  17.6 us
    dot_general x2, matrix products, per_device(): jnp.einsum('cdh,dhnp->chnp', factors, states, precision=lax.Precision.HIG...  9.6 us
    mul x8, local copies, waits for them, and re-layouts, add_level(): per_block = (start_fades * chosen[None]).astype(jnp.bfloat16)  8.65 us
    unnamed x32, local copies, waits for them, and re-layouts  6.36 us
    mul x8, local copies, waits for them, and re-layouts, add_level(): return running + level_scale[:, :, :, None] * projected  6.23 us
    dot_general x1, matrix products, per_device(): jnp.einsum('chij,cjhp->chip', mixing, value_blocks, preferred_element_typ...  5.73 us
  transfers between devices with their start and end apart: 15, of which 13 were waited for; matrix products, arithmetic and copies ran while one was open for 10% of the time, Pallas kernels for 0%

commit v1 on v0

v1 whole, which is shorter than its diff:
```python
import functools

import jax
import jax.numpy as jnp
from jax import lax
from jax.experimental import pallas as pl
from jax.experimental.pallas import tpu as pltpu
from jax.sharding import PartitionSpec as P

MESH = pl.DeviceIdType.MESH
F32 = jnp.float32
BF16 = jnp.bfloat16
SPAN = 256
CHUNK = 128
VMEM = pl.BlockSpec(memory_space=pltpu.VMEM)


def lane(x, index):
    return jnp.broadcast_to(x[:, index : index + 1], x.shape)


def local_kernel(q_ref, k_ref, v_ref, d_ref, w_ref, acc_ref, ext_ref, cum_ref, qt_ref, span_s, half_s, u_s):
    heads, tokens = d_ref.shape
    chunks = tokens // CHUNK
    spans = tokens // SPAN
    rows = lax.broadcasted_iota(jnp.int32, (CHUNK, CHUNK), 0)
    cols = lax.broadcasted_iota(jnp.int32, (CHUNK, CHUNK), 1)
    causal = rows <= cols
    stacked = jnp.concatenate([d_ref[:, m * CHUNK : (m + 1) * CHUNK] for m in range(chunks)], axis=0)
    sums = jnp.dot(stacked, causal.astype(F32), precision=lax.Precision.HIGHEST, preferred_element_type=F32)
    inside = [sums[m * heads : (m + 1) * heads] for m in range(chunks)]
    totals = [lane(x, CHUNK - 1) for x in inside]
    before = jnp.zeros_like(totals[0])
    for m in range(chunks):
        cum_ref[:, m * CHUNK : (m + 1) * CHUNK] = before + inside[m]
        before = before + totals[m]
    span_total = [totals[2 * c] + totals[2 * c + 1] for c in range(spans)]
    qt_ref[...] = q_ref[...].astype(F32).T.astype(BF16)
    for m in range(chunks):
        at = slice(m * CHUNK, (m + 1) * CHUNK)
        c = m // 2
        if m % 2 == 1:
            u_s[0, :, at] = w_ref[0, :, at] * jnp.exp(inside[m])
        else:
            u_s[0, :, at] = jnp.zeros_like(inside[m])
        inner = inside[m] + totals[m - 1] if m % 2 == 1 else inside[m]
        u_s[1, :, at] = w_ref[1, :, at] * jnp.exp(inner)
        u_s[2, :, at] = w_ref[2, :, at] * jnp.exp(inner + span_total[2] if c == 3 else inner)
    for m in range(chunks):
        at = slice(m * CHUNK, (m + 1) * CHUNK)
        c = m // 2
        middle = lane(inside[m], CHUNK // 2 - 1)
        fade_out = jnp.exp(middle - inside[m]).astype(BF16)
        fade_in = w_ref[0, :, at] * jnp.exp(inside[m] - middle)
        rest = jnp.exp(totals[m] - middle)
        chunk_fade = jnp.exp(totals[m])
        keys = k_ref[at, :]
        scores = jnp.dot(keys, qt_ref[:, at], preferred_element_type=F32)
        right = jnp.concatenate([jnp.where(causal, scores, 0.0).astype(BF16), keys], axis=1)
        for h in range(heads):
            vt = v_ref[at, h * 128 : (h + 1) * 128].T
            out = jnp.dot(vt * fade_out[h : h + 1], right, preferred_element_type=F32)
            acc_ref[h, :, at] = out[:, :CHUNK] * fade_in[h : h + 1]
            state = out[:, CHUNK:] * rest[h : h + 1]
            if m % 2 == 0:
                half_s[c, h] = state
            else:
                span_s[c, h] = half_s[c, h] * chunk_fade[h : h + 1] + state
    fades = [jnp.exp(x) for x in span_total]
    all_total = before

    for h in range(heads):
        qt = qt_ref[...]

        def scaled(level, c):
            at = slice(c * SPAN, (c + 1) * SPAN)
            return qt[:, at] * u_s[level, h : h + 1, at].astype(BF16)

        first = span_s[0, h]
        pair = first * fades[1][h : h + 1] + span_s[1, h]
        triple = pair * fades[2][h : h + 1] + span_s[2, h]
        whole = triple * fades[3][h : h + 1] + span_s[3, h]
        ext_ref[h % 2, h // 2, :128] = whole
        ext_ref[h % 2, h // 2, 128:] = jnp.concatenate([all_total] * (8 // heads), axis=0)
        parts = [[], [(1, first)], [(2, pair)], [(1, span_s[2, h]), (2, pair)]]
        for c in range(spans):
            at = slice(c * SPAN, (c + 1) * SPAN)
            items = [(0, half_s[c, h])] + parts[c]
            left = jnp.concatenate([x.astype(BF16) for _, x in items], axis=1)
            right = jnp.concatenate([scaled(level, c) for level, _ in items], axis=0)
            acc_ref[h, :, at] += jnp.dot(left, right, preferred_element_type=F32)


def local_part(queries, keys, values, log_decay, level_weight):
    tokens = queries.shape[0]
    heads = log_decay.shape[0]
    return pl.pallas_call(
        local_kernel,
        out_shape=(
            jax.ShapeDtypeStruct((heads, 128, tokens), F32),
            jax.ShapeDtypeStruct((2, heads // 2, 136, 128), F32),
            jax.ShapeDtypeStruct((heads, tokens), F32),
            jax.ShapeDtypeStruct((128, tokens), BF16),
        ),
        in_specs=[VMEM] * 5,
        out_specs=(VMEM,) * 4,
        scratch_shapes=[
            pltpu.VMEM((tokens // SPAN, heads, 128, 128), F32),
            pltpu.VMEM((tokens // SPAN, heads, 128, 128), F32),
            pltpu.VMEM((3, heads, tokens), F32),
        ],
    )(queries, keys, values, log_decay, level_weight)


def bits_of(n):
    return n.bit_length() - 1


def tree(states, fades):
    found = []
    states, fades = list(states), list(fades)
    while len(states) > 1:
        found.append(states[0::2])
        states = [states[i] * fades[i + 1] + states[i + 1] for i in range(0, len(states), 2)]
        fades = [fades[i] * fades[i + 1] for i in range(0, len(fades), 2)]
    return found, states[0]


def pick(items, index):
    out = items[0]
    for i in range(1, len(items)):
        out = jnp.where(index == i, items[i], out)
    return out


def prefixes(totals, index):
    out = []
    running = jnp.zeros_like(totals[0])
    for bit in range(bits_of(len(totals))):
        out.append(running)
        low = lax.rem(index, 2 ** (bit + 1))
        upper = low >= 2**bit
        start = index - low
        side = jnp.zeros_like(running)
        for i in range(len(totals)):
            inside = jnp.logical_and(i >= start, i < start + 2**bit)
            side = side + jnp.where(inside, totals[i], 0.0)
        running = running + jnp.where(upper, side, 0.0)
    return out, running


def trade_kernel(
    ny, nx, nz, ext_ref, lev_ref, pre_ref,
    r1, gx, hz, lev, lvy, gbuf, hbuf, lvz,
    a_sem, p1_sem, p2_sem, p3_sem, y_sem, x_sem, z_sem, f_sem,
):
    nn = 2 * ny
    by, bx, bz = bits_of(ny), bits_of(nx), bits_of(nz)
    first_x = 1 + by
    first_z = first_x + bx
    part = 128 // nx
    n = lax.axis_index("narrow")
    wide = lax.axis_index("wide")
    y, c = n // 2, lax.rem(n, 2)
    z, x = wide // nx, lax.rem(wide, nx)
    mate = n + 1 - 2 * c

    def copy(src, dst, sems, index, to_n, to_wide):
        return pltpu.make_async_remote_copy(
            src_ref=src, dst_ref=dst, send_sem=sems.at[0, index], recv_sem=sems.at[1, index],
            device_id={"narrow": to_n, "wide": to_wide}, device_id_type=MESH,
        )

    barrier = pltpu.get_barrier_semaphore()
    peers = 0

    def hello(to_n, to_wide):
        pl.semaphore_signal(barrier, inc=1, device_id={"narrow": to_n, "wide": to_wide}, device_id_type=MESH)

    for o in range(1, nn):
        hello(lax.rem(n + o, nn), wide)
        peers += 1
    for o in range(1, nz):
        hello(n, lax.rem(z + o, nz) * nx + x)
        peers += 1
    for ox in range(1, nx):
        for oy in range(ny):
            hello(lax.rem(y + oy, ny) * 2 + c, z * nx + lax.rem(x + ox, nx))
            peers += 1
    pl.semaphore_wait(barrier, peers)

    level0 = copy(ext_ref.at[:, :, pl.ds(0, 128)], lev.at[0], a_sem, 0, mate, wide)

    @pl.when(c == 0)
    def _():
        level0.start()

    def p1(o):
        to = lax.rem(n + o, nn)
        return copy(ext_ref.at[lax.rem(to, 2), to // 2], r1.at[n], p1_sem, o, to, wide)

    for o in range(1, nn):
        p1(o).start()
    r1[n] = ext_ref[c, y]
    for o in range(1, nn):
        source = lax.rem(n + nn - o, nn)
        copy(r1.at[source], r1.at[source], p1_sem, o, n, wide).wait_recv()
    states = [r1[i, :128] for i in range(nn)]
    fades = [jnp.exp(r1[i, pl.ds(128 + n, 1)]) for i in range(nn)]
    narrow_totals = [r1[i, 128:] for i in range(nn)]
    found, group = tree(states, fades)
    gbuf[:128] = group
    group_total = narrow_totals[0]
    for i in range(1, nn):
        group_total = group_total + narrow_totals[i]
    gbuf[128:] = group_total

    def p2(o):
        return copy(gbuf, gx.at[x], p2_sem, o, n, z * nx + lax.rem(x + o, nx))

    for o in range(1, nx):
        p2(o).start()
    slot = 0
    slots = []
    for bit in range(by):
        slots.append(slot)
        for item in found[1 + bit]:
            lvy[slot] = item
            slot += 1

    def y_copy(bit, o):
        to = lax.rem(y + o, ny)
        return copy(
            lvy.at[slots[bit] + to // 2 ** (bit + 1)], lev.at[1 + bit, c, y], y_sem, bit * ny + o, to * 2 + c, wide
        )

    def has(index, bit):
        return lax.rem(index // 2**bit, 2) == 1

    for bit in range(by):
        for o in range(1, ny):

            @pl.when(has(lax.rem(y + o, ny), bit))
            def _():
                y_copy(bit, o).start()

        @pl.when(has(y, bit))
        def _():
            lev[1 + bit, c, y] = lvy[slots[bit] + y // 2 ** (bit + 1)]

        @pl.when(jnp.logical_not(has(y, bit)))
        def _():
            lev[1 + bit] = jnp.zeros(lev.shape[1:], F32)

    @pl.when(c == 0)
    def _():
        lev[0] = jnp.zeros(lev.shape[1:], F32)

    gx[x] = gbuf[...]
    for o in range(1, nx):
        source = lax.rem(x + nx - o, nx)
        copy(gx.at[source], gx.at[source], p2_sem, o, n, wide).wait_recv()
    states = [gx[i, :128] for i in range(nx)]
    fades = [jnp.exp(gx[i, pl.ds(128 + n, 1)]) for i in range(nx)]
    x_totals = [gx[i, 128:] for i in range(nx)]
    found, plane = tree(states, fades)
    hbuf_total = x_totals[0]
    for i in range(1, nx):
        hbuf_total = hbuf_total + x_totals[i]
    gbuf_rows = pl.ds(pl.multiple_of(x * part, part), part)
    r1[0, :128] = plane
    hbuf[:part] = r1[0, gbuf_rows]
    hbuf[part:] = hbuf_total

    def p3(o):
        return copy(hbuf, hz.at[z], p3_sem, o, n, lax.rem(z + o, nz) * nx + x)

    for o in range(1, nz):
        p3(o).start()
    for bit in range(bx):
        value = pick(found[bit], x // 2 ** (bit + 1))
        lev[first_x + bit, c, y] = jnp.where(has(x, bit), value, 0.0)

    def x_copy(o):
        block = lev.at[pl.ds(first_x, bx), c, y]
        return copy(block, block, x_sem, o, lax.rem(y + o, ny) * 2 + c, wide)

    for o in range(1, ny):
        x_copy(o).start()

    def forward(first, count, index):
        block = lev.at[pl.ds(first, count), c]
        return copy(block, block, f_sem, index, mate, wide)

    def forwarded(first, count, index):
        block = lev.at[pl.ds(first, count), 1 - c]
        return copy(block, block, f_sem, index, mate, wide)

    for bit in range(by):

        @pl.when(has(y, bit))
        def _():
            for o in range(1, ny):
                source = lax.rem(y + ny - o, ny)
                block = lev.at[1 + bit, c, source]
                copy(block, block, y_sem, bit * ny + o, n, wide).wait_recv()
            forward(1 + bit, 1, bit).start()

    hz[z] = hbuf[...]
    for o in range(1, nz):
        source = lax.rem(z + nz - o, nz)
        copy(hz.at[source], hz.at[source], p3_sem, o, n, wide).wait_recv()
    states = [hz[i, :part] for i in range(nz)]
    fades = [jnp.exp(hz[i, pl.ds(part + n, 1)]) for i in range(nz)]
    z_totals = [hz[i, part:] for i in range(nz)]
    found, _ = tree(states, fades)
    for bit in range(bz):
        value = pick(found[bit], z // 2 ** (bit + 1))
        lvz[bit] = jnp.where(has(z, bit), value, 0.0)

    def z_block(from_y, from_x):
        return lev.at[pl.ds(first_z, bz), c, from_y, pl.ds(pl.multiple_of(from_x * part, part), part)]

    def z_copy(ox, oy):
        return copy(
            lvz, z_block(y, x), z_sem, ox * ny + oy,
            lax.rem(y + oy, ny) * 2 + c, z * nx + lax.rem(x + ox, nx),
        )

    others = [(ox, oy) for ox in range(nx) for oy in range(ny) if ox or oy]
    for ox, oy in others:
        z_copy(ox, oy).start()
    for bit in range(bz):
        lev[first_z + bit, c, y, gbuf_rows] = lvz[bit]

    for o in range(1, ny):
        block = lev.at[pl.ds(first_x, bx), c, lax.rem(y + ny - o, ny)]
        copy(block, block, x_sem, o, n, wide).wait_recv()
    forward(first_x, bx, by).start()

    low, running = prefixes(narrow_totals, n)
    middle, x_running = prefixes(x_totals, x)
    high, _ = prefixes(z_totals, z)
    for i, item in enumerate(low):
        pre_ref[i] = item[:nn]
    for i, item in enumerate(middle):
        pre_ref[first_x + i] = (running + item)[:nn]
    for i, item in enumerate(high):
        pre_ref[first_z + i] = (running + x_running + item)[:nn]

    for bit in range(by):

        @pl.when(has(y, bit))
        def _():
            forwarded(1 + bit, 1, bit).wait_recv()

    @pl.when(c == 1)
    def _():
        level0.wait_recv()

    forwarded(first_x, bx, by).wait_recv()

    def put(level):
        for h in range(nn):
            lev_ref[h, :, level * 128 : (level + 1) * 128] = lev[level, h % 2, h // 2].astype(BF16)

    for level in range(first_z):
        put(level)
    for ox, oy in others:
        block = z_block(lax.rem(y + ny - oy, ny), lax.rem(x + nx - ox, nx))
        copy(block, block, z_sem, ox * ny + oy, n, wide).wait_recv()
    forward(first_z, bz, by + 1).start()
    forwarded(first_z, bz, by + 1).wait_recv()
    for level in range(first_z, first_z + bz):
        put(level)

    @pl.when(c == 0)
    def _():
        level0.wait_send()

    for o in range(1, nn):
        p1(o).wait_send()
    for o in range(1, nx):
        p2(o).wait_send()
    for o in range(1, nz):
        p3(o).wait_send()
    for o in range(1, ny):
        x_copy(o).wait_send()
    for ox, oy in others:
        z_copy(ox, oy).wait_send()
    for bit in range(by):
        for o in range(1, ny):

            @pl.when(has(lax.rem(y + o, ny), bit))
            def _():
                y_copy(bit, o).wait_send()

        @pl.when(has(y, bit))
        def _():
            forward(1 + bit, 1, bit).wait_send()

    forward(first_x, bx, by).wait_send()
    forward(first_z, bz, by + 1).wait_send()


def trade_part(ext, ny, nx, nz):
    heads = 2 * ny
    levels = 1 + bits_of(ny) + bits_of(nx) + bits_of(nz)
    part = 128 // nx
    dma = pltpu.SemaphoreType.DMA
    return pl.pallas_call(
        functools.partial(trade_kernel, ny, nx, nz),
        out_shape=(
            jax.ShapeDtypeStruct((heads, 128, levels * 128), BF16),
            jax.ShapeDtypeStruct((levels, heads, 128), F32),
        ),
        in_specs=[VMEM],
        out_specs=(VMEM, VMEM),
        scratch_shapes=[
            pltpu.VMEM((heads, 136, 128), F32),
            pltpu.VMEM((nx, 136, 128), F32),
            pltpu.VMEM((nz, part + 8, 128), F32),
            pltpu.VMEM((levels, 2, ny, 128, 128), F32),
            pltpu.VMEM((ny, 128, 128), F32),
            pltpu.VMEM((136, 128), F32),
            pltpu.VMEM((part + 8, 128), F32),
            pltpu.VMEM((bits_of(nz), part, 128), F32),
            dma((2, 1)),
            dma((2, heads)),
            dma((2, nx)),
            dma((2, nz)),
            dma((2, bits_of(ny) * ny)),
            dma((2, ny)),
            dma((2, nx * ny)),
            dma((2, bits_of(ny) + 2)),
        ],
        compiler_params=pltpu.CompilerParams(collective_id=0, has_side_effects=True),
    )(ext)


def finish_kernel(first, qt_ref, lev_ref, pre_ref, cum_ref, w_ref, acc_ref, gain_ref, out_ref):
    heads, tokens = cum_ref.shape
    levels = pre_ref.shape[0]
    gain = gain_ref[...]
    for h in range(heads):
        for c in range(tokens // SPAN):
            at = slice(c * SPAN, (c + 1) * SPAN)
            qt = qt_ref[:, at]
            cum = cum_ref[h : h + 1, at]
            right = []
            for level in range(levels):
                pre = pre_ref[level, h : h + 1, :]
                pre = jnp.concatenate([pre, pre], axis=1)
                scale = w_ref[first + level, h : h + 1, at] * jnp.exp(cum + pre)
                right.append(qt * scale.astype(BF16))
            mixed = acc_ref[h, :, at] + jnp.dot(
                lev_ref[h], jnp.concatenate(right, axis=0), preferred_element_type=F32
            )
            square = jnp.mean(mixed * mixed, axis=0, keepdims=True)
            normed = (mixed * lax.rsqrt(square + 1e-05)).T
            out_ref[at, h * 128 : (h + 1) * 128] = (normed * gain[:, h * 128 : (h + 1) * 128]).astype(BF16)


def finish_part(first, qt, lev, pre, cum, level_weight, acc, gain):
    heads, tokens = cum.shape
    return pl.pallas_call(
        functools.partial(finish_kernel, first),
        out_shape=jax.ShapeDtypeStruct((tokens, heads * 128), BF16),
        in_specs=[VMEM] * 7,
        out_specs=VMEM,
    )(qt, lev, pre, cum, level_weight, acc, gain)


def per_device(sizes, queries, keys, values, log_decay, level_weight, norm_gain):
    ny, nx, nz = sizes
    acc, ext, cum, qt = local_part(queries, keys, values, log_decay, level_weight)
    lev, pre = trade_part(ext, ny, nx, nz)
    first = level_weight.shape[0] - pre.shape[0]
    return finish_part(first, qt, lev, pre, cum, level_weight, acc, norm_gain.reshape(1, -1))


def solution(mesh, nx=4):
    sizes = (mesh.shape["narrow"] // 2, nx, mesh.shape["wide"] // nx)
    placed = (
        P(("wide", "narrow"), None),
        P(("wide", "narrow"), None),
        P(("wide", "narrow"), None),
        P(None, ("wide", "narrow")),
        P(None, None, ("wide", "narrow")),
        P(),
    )
    return jax.shard_map(
        functools.partial(per_device, sizes),
        mesh=mesh,
        in_specs=placed,
        out_specs=P(("wide", "narrow"), None),
        check_vma=False,
    )
```

time: 218 us -> 64 us (0.29)
  the two profiles are of different devices: /device:TPU:230 before, /device:TPU:1 now
where the time goes in v1:
time: 64 us; the launch traced here: 63.9 us
  Pallas kernels  63.8 us (100%)
    pallas_call x1, Pallas kernels, trade_part(): pl.pallas_call(functools.partial(trade_kernel, ny, nx, nz), out_shape=(ja...  48.5 us
    pallas_call x1, Pallas kernels, finish_part(): pl.pallas_call(functools.partial(finish_kernel, first), out_shape=jax.Sha...  8.06 us
    pallas_call x1, Pallas kernels, local_part(): pl.pallas_call(local_kernel, out_shape=(jax.ShapeDtypeStruct((heads, 128,...  7.25 us

profile of v1, /device:TPU:1, one launch (start us, length us, event | category | flops | bytes accessed | tf_op | source)
XLA Modules:
  0.0 63.9 jit_solution(17830728845864264475)
XLA Ops:
  0.0 7.3 %shard_map.64 = (f32[8,128,1024]{2,1,0:T(8,128)}, f32[2,4,136,128]{3,2,1,0:T(8,128)}, f32[8,1024]{1,0:T(8,128)}, bf16[128,1024]{1,0:T(8,128)(2,1)}) custom-call(bf16[1024,128]{1,0:T(8,128)(2,1)} %q_ref.1, bf16[1024,128]{1,0:T(8,128)(2,1)} %k_ref.1, bf16[1024,1024]{1,0:T(8,128)(2,1)} %v_ref.1, f32[8,1024]{1,0:T(8,128)} %d_ref.1, f32[11,8,1024]{2,1,0:T(8,128)} %w_ref.3), custom_call_target="tpu_custom_call" | custom-call | tf_op jit(solution)/shard_map/pallas_call | solution.py:97
  7.3 48.5 %shard_map.65 = (bf16[8,128,1024]{2,1,0:T(8,128)(2,1)}, f32[8,8,128]{2,1,0:T(8,128)}) custom-call(f32[2,4,136,128]{3,2,1,0:T(8,128)} %get-tuple-element.12.ext_ref), custom_call_target="tpu_custom_call" | custom-call | tf_op jit(solution)/shard_map/pallas_call | solution.py:411
  55.8 8.1 %shard_map.66 = bf16[1024,1024]{1,0:T(8,128)(2,1)} custom-call(bf16[128,1024]{1,0:T(8,128)(2,1)} %get-tuple-element.11.qt_ref, bf16[8,128,1024]{2,1,0:T(8,128)(2,1)} %get-tuple-element.13.lev_ref, f32[8,8,128]{2,1,0:T(8,128)} %get-tuple-element.14.pre_ref, f32[8,1024]{1,0:T(8,128)} %get-tuple-element.15.cum_ref, f32[11,8,1024]{2,1,0:T(8,128)} %w_ref.3, ...), custom_call_target="tpu_custom_call" | custom-call | tf_op jit(solution)/shard_map/pallas_call | solution.py:466

commit v2 on v1

v2 whole, which is shorter than its diff:
```python
import functools

import jax
import jax.numpy as jnp
from jax import lax
from jax.experimental import pallas as pl
from jax.experimental.pallas import tpu as pltpu
from jax.sharding import PartitionSpec as P

MESH = pl.DeviceIdType.MESH
F32 = jnp.float32
BF16 = jnp.bfloat16
SPAN = 256
CHUNK = 128
VMEM = pl.BlockSpec(memory_space=pltpu.VMEM)


def lane(x, index):
    return jnp.broadcast_to(x[:, index : index + 1], x.shape)


def columns(index, width):
    return pl.ds(pl.multiple_of(index * width, width), width)


def bits_of(n):
    return n.bit_length() - 1


def tree(states, fades):
    found = []
    states, fades = list(states), list(fades)
    while len(states) > 1:
        found.append(states[0::2])
        states = [states[i] * fades[i + 1] + states[i + 1] for i in range(0, len(states), 2)]
        fades = [fades[i] * fades[i + 1] for i in range(0, len(fades), 2)]
    return found, states[0]


def pick(items, index):
    out = items[0]
    for i in range(1, len(items)):
        out = jnp.where(index == i, items[i], out)
    return out


def prefixes(totals, index):
    out = []
    running = jnp.zeros_like(totals[0])
    for bit in range(bits_of(len(totals))):
        out.append(running)
        low = lax.rem(index, 2 ** (bit + 1))
        upper = low >= 2**bit
        start = index - low
        side = jnp.zeros_like(running)
        for i in range(len(totals)):
            inside = jnp.logical_and(i >= start, i < start + 2**bit)
            side = side + jnp.where(inside, totals[i], 0.0)
        running = running + jnp.where(upper, side, 0.0)
    return out, running


def main_kernel(
    ny, nx, nz, q_hbm, k_hbm, v_hbm, d_hbm, w_hbm, acc_ref, lev_ref, pre_ref, cum_ref, qt_ref,
    ext, mate_buf, chip_buf, r1, gq, gxq, gbuf, gx, hbuf, hz, lev, lvy, lvz, rights, span_s, half_s, rows_s, u_s,
    e_sem, a_sem, p1_sem, p2_sem, g_sem, p3_sem, y_sem, x_sem, z_sem, f_sem, in_sem,
    q_ref, k_ref, v_ref, d_ref, w_ref,
):
    heads, tokens = d_ref.shape
    chunks, spans = tokens // CHUNK, tokens // SPAN
    local = bits_of(spans)
    by, bx, bz = bits_of(ny), bits_of(nx), bits_of(nz)
    first_x = 1 + by
    first_z = first_x + bx
    part = 128 // nx
    n = lax.axis_index("narrow")
    wide = lax.axis_index("wide")
    y, c = n // 2, lax.rem(n, 2)
    z, x = wide // nx, lax.rem(wide, nx)
    mate = n + 1 - 2 * c
    own_rows = pl.ds(pl.multiple_of(x * part, part), part)

    def copy(src, dst, sems, index, to_n, to_wide):
        return pltpu.make_async_remote_copy(
            src_ref=src, dst_ref=dst, send_sem=sems.at[0, index], recv_sem=sems.at[1, index],
            device_id={"narrow": to_n, "wide": to_wide}, device_id_type=MESH,
        )

    def has(index, bit):
        return lax.rem(index // 2**bit, 2) == 1

    fetches = [
        pltpu.make_async_copy(src, dst, in_sem.at[i])
        for i, (src, dst) in enumerate(
            [(d_hbm, d_ref), (k_hbm, k_ref), (v_hbm, v_ref), (q_hbm, q_ref), (w_hbm, w_ref)]
        )
    ]
    for fetch in fetches:
        fetch.start()

    barrier = pltpu.get_barrier_semaphore()
    peers = 0

    def hello(to_n, to_wide):
        pl.semaphore_signal(barrier, inc=1, device_id={"narrow": to_n, "wide": to_wide}, device_id_type=MESH)

    for o in range(1, nz):
        hello(n, lax.rem(z + o, nz) * nx + x)
        peers += 1
    for ox in range(nx):
        for oy in range(ny):
            if ox or oy:
                hello(lax.rem(y + oy, ny) * 2 + c, z * nx + lax.rem(x + ox, nx))
                peers += 1
    hello(mate, wide)
    peers += 1

    fetches[0].wait()
    at = [slice(m * CHUNK, (m + 1) * CHUNK) for m in range(chunks)]
    causal = lax.broadcasted_iota(jnp.int32, (CHUNK, CHUNK), 0) <= lax.broadcasted_iota(jnp.int32, (CHUNK, CHUNK), 1)
    stacked = jnp.concatenate([d_ref[:, at[m]] for m in range(chunks)], axis=0)
    sums = jnp.dot(stacked, causal.astype(F32), precision=lax.Precision.HIGHEST, preferred_element_type=F32)
    inside = [sums[m * heads : (m + 1) * heads] for m in range(chunks)]
    totals = [lane(v, CHUNK - 1) for v in inside]
    before = jnp.zeros_like(totals[0])
    for m in range(chunks):
        cum_ref[:, at[m]] = before + inside[m]
        before = before + totals[m]
    own_total = jnp.concatenate([before] * (8 // heads), axis=0)
    after = jnp.zeros_like(before)
    fades = [None] * chunks
    for m in reversed(range(chunks)):
        fades[m] = jnp.exp(after + (totals[m] - inside[m]))
        after = after + totals[m]

    fetches[1].wait()
    kt = k_ref[...].astype(F32).T
    fade = jnp.concatenate(fades, axis=1)
    fetches[2].wait()
    for h in range(heads):
        keys = (kt * fade[h : h + 1]).astype(BF16)
        state = jnp.dot(keys, v_ref[:, h * 128 : (h + 1) * 128], preferred_element_type=F32)
        ext[h % 2, h // 2, :128] = state.T
        ext[h % 2, h // 2, 128:] = own_total

    pl.semaphore_wait(barrier, peers)

    swap = copy(ext.at[1 - c], mate_buf, e_sem, 0, mate, wide)
    swap.start()
    level0 = copy(ext.at[:, :, pl.ds(0, 128)], lev.at[0], a_sem, 0, mate, wide)

    @pl.when(c == 0)
    def _():
        level0.start()

    @pl.when(c == 0)
    def _():
        lev[0] = jnp.zeros(lev.shape[1:], F32)

    swap.wait_recv()
    mate_total = mate_buf[0, 128:]
    for j in range(ny):
        mine = ext[c, j]
        theirs = mate_buf[j]
        row = pl.ds(128 + 2 * j + c, 1)
        left = jnp.where(c == 0, jnp.exp(mate_buf[j, row]), 1.0)
        right = jnp.where(c == 0, 1.0, jnp.exp(ext[c, j, row]))
        chip_buf[j, :128] = mine[:128] * left + theirs[:128] * right
        chip_buf[j, 128:] = mine[128:] + theirs[128:]

    def p1(o):
        to = lax.rem(y + o, ny)
        return copy(chip_buf.at[to], r1.at[y], p1_sem, o, to * 2 + c, wide)

    for o in range(1, ny):
        p1(o).start()

    fetches[3].wait()
    fetches[4].wait()
    qt_ref[...] = q_ref[...].astype(F32).T
    for m in range(chunks):
        keys = k_ref[at[m], :]
        scores = jnp.dot(keys, qt_ref[:, at[m]].astype(BF16), preferred_element_type=F32)
        rights[m] = jnp.concatenate([jnp.where(causal, scores, 0.0).astype(BF16), keys], axis=1)
        middle = lane(inside[m], CHUNK // 2 - 1)
        rows_s[0, :, at[m]] = jnp.exp(middle - inside[m])
        rows_s[1, :, at[m]] = w_ref[0, :, at[m]] * jnp.exp(inside[m] - middle)
        rows_s[2, :, at[m]] = jnp.exp(totals[m] - middle)
        rows_s[3, :, at[m]] = jnp.exp(totals[m])
    span_total = [totals[2 * i] + totals[2 * i + 1] for i in range(spans)]
    for m in range(chunks):
        inner = inside[m] + totals[m - 1] if m % 2 == 1 else inside[m]
        u_s[0, :, at[m]] = w_ref[0, :, at[m]] * jnp.exp(inside[m]) if m % 2 == 1 else jnp.zeros_like(inner)
        u_s[1, :, at[m]] = w_ref[1, :, at[m]] * jnp.exp(inner)
        u_s[2, :, at[m]] = w_ref[2, :, at[m]] * jnp.exp(inner + span_total[2] if m // 2 == 3 else inner)

    def chunk_products(h, carry):
        one = pl.ds(h, 1)
        out_row, in_row, rest_row, whole_row = [rows_s[i, one, :] for i in range(4)]
        for m in range(chunks):
            vt = v_ref[at[m], columns(h, 128)].T.astype(F32)
            left = (vt * out_row[:, at[m]]).astype(BF16)
            out = jnp.dot(left, rights[m], preferred_element_type=F32)
            acc_ref[h, :, at[m]] = out[:, :CHUNK] * in_row[:, at[m]]
            state = out[:, CHUNK:] * rest_row[:, at[m]]
            if m % 2 == 0:
                half_s[m // 2, h] = state
            else:
                span_s[m // 2, h] = half_s[m // 2, h] * whole_row[:, at[m]] + state
        return carry

    lax.fori_loop(0, heads, chunk_products, 0)

    r1[y] = chip_buf[y]
    for o in range(1, ny):
        source = lax.rem(y + ny - o, ny)
        copy(r1.at[source], r1.at[source], p1_sem, o, n, wide).wait_recv()
    chip_totals = [r1[i, 128:] for i in range(ny)]
    found, group = tree([r1[i, :128] for i in range(ny)], [jnp.exp(r1[i, pl.ds(128 + n, 1)]) for i in range(ny)])
    group_total = chip_totals[0]
    for i in range(1, ny):
        group_total = group_total + chip_totals[i]
    for i in range(nx):
        gq[i, :part] = group[i * part : (i + 1) * part]
        gq[i, part:] = group_total
    gbuf[...] = group

    def p2(o):
        to = lax.rem(x + o, nx)
        return copy(gq.at[to], gxq.at[x], p2_sem, o, n, z * nx + to)

    def whole_x(o):
        return copy(gbuf, gx.at[x], g_sem, o, n, z * nx + lax.rem(x + o, nx))

    for o in range(1, nx):
        p2(o).start()
    for o in range(1, nx):
        whole_x(o).start()
    slot = 0
    slots = []
    for bit in range(by):
        slots.append(slot)
        for item in found[bit]:
            lvy[slot] = item
            slot += 1

    def y_copy(bit, o):
        to = lax.rem(y + o, ny)
        return copy(
            lvy.at[slots[bit] + to // 2 ** (bit + 1)], lev.at[1 + bit, c, y], y_sem, bit * ny + o, to * 2 + c, wide
        )

    for bit in range(by):
        for o in range(1, ny):

            @pl.when(has(lax.rem(y + o, ny), bit))
            def _():
                y_copy(bit, o).start()

        @pl.when(has(y, bit))
        def _():
            lev[1 + bit, c, y] = lvy[slots[bit] + y // 2 ** (bit + 1)]

        @pl.when(jnp.logical_not(has(y, bit)))
        def _():
            lev[1 + bit] = jnp.zeros(lev.shape[1:], F32)

    gxq[x] = gq[x]
    gx[x] = gbuf[...]
    for o in range(1, nx):
        source = lax.rem(x + nx - o, nx)
        copy(gxq.at[source], gxq.at[source], p2_sem, o, n, wide).wait_recv()
    x_totals = [gxq[i, part:] for i in range(nx)]
    x_fades = [jnp.exp(gxq[i, pl.ds(part + n, 1)]) for i in range(nx)]
    _, plane = tree([gxq[i, :part] for i in range(nx)], x_fades)
    plane_total = x_totals[0]
    for i in range(1, nx):
        plane_total = plane_total + x_totals[i]
    hbuf[:part] = plane
    hbuf[part:] = plane_total

    def p3(o):
        return copy(hbuf, hz.at[z], p3_sem, o, n, lax.rem(z + o, nz) * nx + x)

    for o in range(1, nz):
        p3(o).start()

    for o in range(1, nx):
        source = lax.rem(x + nx - o, nx)
        copy(gx.at[source], gx.at[source], g_sem, o, n, wide).wait_recv()
    found, _ = tree([gx[i] for i in range(nx)], x_fades)
    for bit in range(bx):
        value = pick(found[bit], x // 2 ** (bit + 1))
        lev[first_x + bit, c, y] = jnp.where(has(x, bit), value, 0.0)

    def x_copy(o):
        block = lev.at[pl.ds(first_x, bx), c, y]
        return copy(block, block, x_sem, o, lax.rem(y + o, ny) * 2 + c, wide)

    for o in range(1, ny):
        x_copy(o).start()

    def forward(first, count, index):
        block = lev.at[pl.ds(first, count), c]
        return copy(block, block, f_sem, index, mate, wide)

    def forwarded(first, count, index):
        block = lev.at[pl.ds(first, count), 1 - c]
        return copy(block, block, f_sem, index, mate, wide)

    for bit in range(by):

        @pl.when(has(y, bit))
        def _():
            for o in range(1, ny):
                source = lax.rem(y + ny - o, ny)
                block = lev.at[1 + bit, c, source]
                copy(block, block, y_sem, bit * ny + o, n, wide).wait_recv()
            forward(1 + bit, 1, bit).start()

    hz[z] = hbuf[...]
    for o in range(1, nz):
        source = lax.rem(z + nz - o, nz)
        copy(hz.at[source], hz.at[source], p3_sem, o, n, wide).wait_recv()
    z_totals = [hz[i, part:] for i in range(nz)]
    found, _ = tree([hz[i, :part] for i in range(nz)], [jnp.exp(hz[i, pl.ds(part + n, 1)]) for i in range(nz)])
    for bit in range(bz):
        value = pick(found[bit], z // 2 ** (bit + 1))
        lvz[bit] = jnp.where(has(z, bit), value, 0.0)

    def z_block(from_y, from_x):
        return lev.at[pl.ds(first_z, bz), c, from_y, pl.ds(pl.multiple_of(from_x * part, part), part)]

    def z_copy(ox, oy):
        return copy(
            lvz, z_block(y, x), z_sem, ox * ny + oy,
            lax.rem(y + oy, ny) * 2 + c, z * nx + lax.rem(x + ox, nx),
        )

    others = [(ox, oy) for ox in range(nx) for oy in range(ny) if ox or oy]
    for ox, oy in others:
        z_copy(ox, oy).start()
    for bit in range(bz):
        lev[first_z + bit, c, y, own_rows] = lvz[bit]

    def local_levels(h, carry):
        one = pl.ds(h, 1)
        whole_row = rows_s[3, one, :]
        scales = [u_s[level, one, :] for level in range(3)]
        first = span_s[0, h]
        pair = first * (whole_row[:, at[2]] * whole_row[:, at[3]]) + span_s[1, h]
        parts = [[], [(1, first)], [(2, pair)], [(1, span_s[2, h]), (2, pair)]]
        for i in range(spans):
            here = slice(i * SPAN, (i + 1) * SPAN)
            items = [(0, half_s[i, h])] + parts[i]
            left = jnp.concatenate([v.astype(BF16) for _, v in items], axis=1)
            right = jnp.concatenate(
                [(qt_ref[:, here] * scales[level][:, here]).astype(BF16) for level, _ in items], axis=0
            )
            acc_ref[h, :, here] += jnp.dot(left, right, preferred_element_type=F32)
        return carry

    lax.fori_loop(0, heads, local_levels, 0)

    for o in range(1, ny):
        block = lev.at[pl.ds(first_x, bx), c, lax.rem(y + ny - o, ny)]
        copy(block, block, x_sem, o, n, wide).wait_recv()
    forward(first_x, bx, by).start()

    low = jnp.where(c == 1, mate_total, 0.0)
    chip_pre, y_running = prefixes(chip_totals, y)
    middle, x_running = prefixes(x_totals, x)
    high, _ = prefixes(z_totals, z)
    base = low + y_running
    pres = [jnp.zeros_like(low)] + [low + v for v in chip_pre]
    pres += [base + v for v in middle] + [base + x_running + v for v in high]
    for level, pre in enumerate(pres):
        pre_ref[level] = pre[:heads]
    for level in range(first_z):
        wide_pre = jnp.concatenate([pres[level][:heads]] * chunks, axis=1)
        u_s[1 + local + level] = w_ref[1 + local + level] * jnp.exp(cum_ref[...] + wide_pre)

    for bit in range(by):

        @pl.when(has(y, bit))
        def _():
            forwarded(1 + bit, 1, bit).wait_recv()

    @pl.when(c == 1)
    def _():
        level0.wait_recv()

    forwarded(first_x, bx, by).wait_recv()

    def outer_levels(h, carry):
        one = pl.ds(h, 1)
        left = jnp.concatenate(
            [lev[level, lax.rem(h, 2), h // 2].astype(BF16) for level in range(first_z)], axis=1
        )
        scales = [u_s[1 + local + level, one, :] for level in range(first_z)]
        for i in range(spans):
            here = slice(i * SPAN, (i + 1) * SPAN)
            right = jnp.concatenate(
                [(qt_ref[:, here] * scales[level][:, here]).astype(BF16) for level in range(first_z)], axis=0
            )
            acc_ref[h, :, here] += jnp.dot(left, right, preferred_element_type=F32)
        return carry

    lax.fori_loop(0, heads, outer_levels, 0)

    for ox, oy in others:
        block = z_block(lax.rem(y + ny - oy, ny), lax.rem(x + nx - ox, nx))
        copy(block, block, z_sem, ox * ny + oy, n, wide).wait_recv()
    forward(first_z, bz, by + 1).start()

    swap.wait_send()

    @pl.when(c == 0)
    def _():
        level0.wait_send()

    for o in range(1, ny):
        p1(o).wait_send()
        x_copy(o).wait_send()
    for o in range(1, nx):
        p2(o).wait_send()
        whole_x(o).wait_send()
    for o in range(1, nz):
        p3(o).wait_send()
    for ox, oy in others:
        z_copy(ox, oy).wait_send()
    for bit in range(by):
        for o in range(1, ny):

            @pl.when(has(lax.rem(y + o, ny), bit))
            def _():
                y_copy(bit, o).wait_send()

        @pl.when(has(y, bit))
        def _():
            forward(1 + bit, 1, bit).wait_send()

    forward(first_x, bx, by).wait_send()
    forwarded(first_z, bz, by + 1).wait_recv()
    for level in range(bz):
        for h in range(heads):
            lev_ref[h, :, level * 128 : (level + 1) * 128] = lev[first_z + level, h % 2, h // 2].astype(BF16)
    forward(first_z, bz, by + 1).wait_send()


def main_part(ny, nx, nz, queries, keys, values, log_decay, level_weight):
    heads, tokens = log_decay.shape
    by, bx, bz = bits_of(ny), bits_of(nx), bits_of(nz)
    levels = 1 + by + bx + bz
    chunks, spans = tokens // CHUNK, tokens // SPAN
    part = 128 // nx
    dma = pltpu.SemaphoreType.DMA
    return pl.pallas_call(
        functools.partial(main_kernel, ny, nx, nz),
        out_shape=(
            jax.ShapeDtypeStruct((heads, 128, tokens), F32),
            jax.ShapeDtypeStruct((heads, 128, bz * 128), BF16),
            jax.ShapeDtypeStruct((levels, heads, 128), F32),
            jax.ShapeDtypeStruct((heads, tokens), F32),
            jax.ShapeDtypeStruct((128, tokens), F32),
        ),
        in_specs=[pl.BlockSpec(memory_space=pltpu.HBM)] * 5,
        out_specs=(VMEM,) * 5,
        scratch_shapes=[
            pltpu.VMEM((2, ny, 136, 128), F32),
            pltpu.VMEM((ny, 136, 128), F32),
            pltpu.VMEM((ny, 136, 128), F32),
            pltpu.VMEM((ny, 136, 128), F32),
            pltpu.VMEM((nx, part + 8, 128), F32),
            pltpu.VMEM((nx, part + 8, 128), F32),
            pltpu.VMEM((128, 128), F32),
            pltpu.VMEM((nx, 128, 128), F32),
            pltpu.VMEM((part + 8, 128), F32),
            pltpu.VMEM((nz, part + 8, 128), F32),
            pltpu.VMEM((levels, 2, ny, 128, 128), F32),
            pltpu.VMEM((ny, 128, 128), F32),
            pltpu.VMEM((bz, part, 128), F32),
            pltpu.VMEM((chunks, CHUNK, 2 * CHUNK), BF16),
            pltpu.VMEM((spans, heads, 128, 128), F32),
            pltpu.VMEM((spans, heads, 128, 128), F32),
            pltpu.VMEM((4, heads, tokens), F32),
            pltpu.VMEM((1 + bits_of(spans) + 1 + by + bx, heads, tokens), F32),
            dma((2, 1)),
            dma((2, 1)),
            dma((2, ny)),
            dma((2, nx)),
            dma((2, nx)),
            dma((2, nz)),
            dma((2, by * ny)),
            dma((2, ny)),
            dma((2, nx * ny)),
            dma((2, by + 2)),
            dma((5,)),
            pltpu.VMEM(queries.shape, queries.dtype),
            pltpu.VMEM(keys.shape, keys.dtype),
            pltpu.VMEM(values.shape, values.dtype),
            pltpu.VMEM(log_decay.shape, log_decay.dtype),
            pltpu.VMEM(level_weight.shape, level_weight.dtype),
        ],
        compiler_params=pltpu.CompilerParams(collective_id=0, has_side_effects=True, vmem_limit_bytes=40 * 2**20),
    )(*[pltpu.with_memory_space_constraint(v, pltpu.HBM) for v in (queries, keys, values, log_decay, level_weight)])


def finish_kernel(skip, qt_ref, lev_ref, pre_ref, cum_ref, w_ref, acc_ref, gain_ref, out_ref):
    heads, tokens = cum_ref.shape
    levels = lev_ref.shape[2] // 128
    first = w_ref.shape[0] - levels
    gain = gain_ref[...]
    for h in range(heads):
        for i in range(tokens // SPAN):
            at = slice(i * SPAN, (i + 1) * SPAN)
            qt = qt_ref[:, at]
            cum = cum_ref[h : h + 1, at]
            right = []
            for level in range(levels):
                pre = pre_ref[skip + level, h : h + 1, :]
                pre = jnp.concatenate([pre, pre], axis=1)
                right.append((qt * (w_ref[first + level, h : h + 1, at] * jnp.exp(cum + pre))).astype(BF16))
            mixed = acc_ref[h, :, at] + jnp.dot(
                lev_ref[h], jnp.concatenate(right, axis=0), preferred_element_type=F32
            )
            square = jnp.mean(mixed * mixed, axis=0, keepdims=True)
            normed = (mixed * lax.rsqrt(square + 1e-05)).T
            out_ref[at, h * 128 : (h + 1) * 128] = (normed * gain[:, h * 128 : (h + 1) * 128]).astype(BF16)


def finish_part(skip, qt, lev, pre, cum, level_weight, acc, gain):
    heads, tokens = cum.shape
    return pl.pallas_call(
        functools.partial(finish_kernel, skip),
        out_shape=jax.ShapeDtypeStruct((tokens, heads * 128), BF16),
        in_specs=[VMEM] * 7,
        out_specs=VMEM,
        compiler_params=pltpu.CompilerParams(vmem_limit_bytes=24 * 2**20),
    )(qt, lev, pre, cum, level_weight, acc, gain)


def per_device(sizes, queries, keys, values, log_decay, level_weight, norm_gain):
    ny, nx, nz = sizes
    acc, lev, pre, cum, qt = main_part(ny, nx, nz, queries, keys, values, log_decay, level_weight)
    skip = pre.shape[0] - lev.shape[2] // 128
    return finish_part(skip, qt, lev, pre, cum, level_weight, acc, norm_gain.reshape(1, -1))


def solution(mesh, nx=4):
    sizes = (mesh.shape["narrow"] // 2, nx, mesh.shape["wide"] // nx)
    placed = (
        P(("wide", "narrow"), None),
        P(("wide", "narrow"), None),
        P(("wide", "narrow"), None),
        P(None, ("wide", "narrow")),
        P(None, None, ("wide", "narrow")),
        P(),
    )
    return jax.shard_map(
        functools.partial(per_device, sizes),
        mesh=mesh,
        in_specs=placed,
        out_specs=P(("wide", "narrow"), None),
        check_vma=False,
    )
```

time: 64 us -> 51.3 us (0.80)
  Pallas kernels: 63.8 us -> 51.2 us
    pallas_call x3 -> x2, Pallas kernels: 63.8 us -> 51.2 us  [the longest x1 47.5 us: main_part(): pl.pallas_call(functools.partial(main_kernel, ny, nx, nz), out_shape=(jax...]
where the time goes in v2:
time: 51.3 us
  Pallas kernels  51.2 us (100%)
    pallas_call x1, Pallas kernels, main_part(): pl.pallas_call(functools.partial(main_kernel, ny, nx, nz), out_shape=(jax...  47.5 us
    pallas_call x1, Pallas kernels, finish_part(): pl.pallas_call(functools.partial(finish_kernel, skip), out_shape=jax.Shap...  3.71 us

profile of v2, /device:TPU:1, one launch (start us, length us, event | category | flops | bytes accessed | tf_op | source)
XLA Modules:
  0.0 51.3 jit_solution(9469087832214954684)
XLA Ops:
  0.0 0.0 copy-start
  0.0 0.0 copy-start.1
  0.0 47.5 %shard_map.64 = (f32[8,128,1024]{2,1,0:T(8,128)S(1)}, bf16[8,128,384]{2,1,0:T(8,128)(2,1)S(1)}, f32[8,8,128]{2,1,0:T(8,128)S(1)}, f32[8,1024]{1,0:T(8,128)S(1)}, f32[128,1024]{1,0:T(8,128)S(1)}) custom-call(bf16[1024,128]{1,0:T(8,128)(2,1)} %q_hbm.1, bf16[1024,128]{1,0:T(8,128)(2,1)} %k_hbm.1, bf16[1024,1024]{1,0:T(8,128)(2,1)} %v_hbm.1, f32[8,1024]{1,0:T(8,128)} %d_hbm.1, ...), custom_call_target="tpu_custom_call" | custom-call | tf_op jit(solution)/shard_map/pallas_call | solution.py:458
  47.5 0.0 copy-done
  47.5 0.0 copy-done.1
  47.6 3.7 %shard_map.65 = bf16[1024,1024]{1,0:T(8,128)(2,1)} custom-call(f32[128,1024]{1,0:T(8,128)S(1)} %get-tuple-element.10.qt_ref, bf16[8,128,384]{2,1,0:T(8,128)(2,1)S(1)} %get-tuple-element.11.lev_ref, f32[8,8,128]{2,1,0:T(8,128)S(1)} %get-tuple-element.12.pre_ref, f32[8,1024]{1,0:T(8,128)S(1)} %get-tuple-element.13.cum_ref, f32[11,8,1024]{2,1,0:T(8,128)S(1)} %copy-done, ...), custom_call_target="tpu_custom_call" | custom-call | tf_op jit(solution)/shard_map/pallas_call | solution.py:534
Async XLA Ops:
  0.0 47.5 %copy-start = (f32[11,8,1024]{2,1,0:T(8,128)S(1)}, f32[11,8,1024]{2,1,0:T(8,128)}, u32[]{:S(2)}) copy-start(f32[11,8,1024]{2,1,0:T(8,128)} %w_ref.1) | copy-start | bytes 1081348
  0.0 47.5 %copy-start.1 = (f32[1024]{0:T(1024)S(1)}, f32[1024]{0:T(1024)}, u32[]{:S(2)}) copy-start(f32[1024]{0:T(1024)} %param.11) | copy-start | bytes 12292

commit v3 on v2

--- a/solution.py
+++ b/solution.py
@@ -61,8 +61,8 @@
 
 
 def main_kernel(
-    ny, nx, nz, q_hbm, k_hbm, v_hbm, d_hbm, w_hbm, acc_ref, lev_ref, pre_ref, cum_ref, qt_ref,
-    ext, mate_buf, chip_buf, r1, gq, gxq, gbuf, gx, hbuf, hz, lev, lvy, lvz, rights, span_s, half_s, rows_s, u_s,
+    ny, nx, nz, q_hbm, k_hbm, v_hbm, d_hbm, w_hbm, gain_hbm, acc_ref, lev_ref, right_ref, gain_ref,
+    ext, mate_buf, chip_buf, r1, gq, gxq, gbuf, gx, hbuf, hz, lev, lvy, lvz, rights, span_s, half_s, rows_s, u_s, cum_ref, qt_ref, fade_s,
     e_sem, a_sem, p1_sem, p2_sem, g_sem, p3_sem, y_sem, x_sem, z_sem, f_sem, in_sem,
     q_ref, k_ref, v_ref, d_ref, w_ref,
 ):
@@ -92,7 +92,10 @@
     fetches = [
         pltpu.make_async_copy(src, dst, in_sem.at[i])
         for i, (src, dst) in enumerate(
-            [(d_hbm, d_ref), (k_hbm, k_ref), (v_hbm, v_ref), (q_hbm, q_ref), (w_hbm, w_ref)]
+            [
+                (d_hbm, d_ref), (k_hbm, k_ref), (v_hbm, v_ref), (q_hbm, q_ref), (w_hbm, w_ref),
+                (gain_hbm, gain_ref),
+            ]
         )
     ]
     for fetch in fetches:
@@ -105,8 +108,11 @@
         pl.semaphore_signal(barrier, inc=1, device_id={"narrow": to_n, "wide": to_wide}, device_id_type=MESH)
 
     for o in range(1, nz):
-        hello(n, lax.rem(z + o, nz) * nx + x)
-        peers += 1
+
+        @pl.when(z >= o)
+        def _():
+            hello(n, (z - o) * nx + x)
+
     for ox in range(nx):
         for oy in range(ny):
             if ox or oy:
@@ -135,18 +141,23 @@
 
     fetches[1].wait()
     kt = k_ref[...].astype(F32).T
-    fade = jnp.concatenate(fades, axis=1)
+    for m in range(chunks):
+        fade_s[:, at[m]] = fades[m]
     fetches[2].wait()
-    for h in range(heads):
-        keys = (kt * fade[h : h + 1]).astype(BF16)
-        state = jnp.dot(keys, v_ref[:, h * 128 : (h + 1) * 128], preferred_element_type=F32)
-        ext[h % 2, h // 2, :128] = state.T
-        ext[h % 2, h // 2, 128:] = own_total
-
-    pl.semaphore_wait(barrier, peers)
-
+
+    def states(odd):
+        for j in range(ny):
+            h = 2 * j + odd
+            keys = (kt * fade_s[pl.ds(h, 1), :]).astype(BF16)
+            state = jnp.dot(keys, v_ref[:, columns(h, 128)], preferred_element_type=F32)
+            ext[odd, j, :128] = state.T
+            ext[odd, j, 128:] = own_total
+
+    states(1 - c)
+    pl.semaphore_wait(barrier, peers + nz - 1 - z)
     swap = copy(ext.at[1 - c], mate_buf, e_sem, 0, mate, wide)
     swap.start()
+    states(c)
     level0 = copy(ext.at[:, :, pl.ds(0, 128)], lev.at[0], a_sem, 0, mate, wide)
 
     @pl.when(c == 0)
@@ -177,6 +188,7 @@
 
     fetches[3].wait()
     fetches[4].wait()
+    fetches[5].wait()
     qt_ref[...] = q_ref[...].astype(F32).T
     for m in range(chunks):
         keys = k_ref[at[m], :]
@@ -280,25 +292,34 @@
     hbuf[part:] = plane_total
 
     def p3(o):
-        return copy(hbuf, hz.at[z], p3_sem, o, n, lax.rem(z + o, nz) * nx + x)
+        return copy(hbuf, hz.at[z], p3_sem, o, n, (z + o) * nx + x)
 
     for o in range(1, nz):
-        p3(o).start()
+
+        @pl.when(z + o < nz)
+        def _():
+            p3(o).start()
 
     for o in range(1, nx):
         source = lax.rem(x + nx - o, nx)
         copy(gx.at[source], gx.at[source], g_sem, o, n, wide).wait_recv()
     found, _ = tree([gx[i] for i in range(nx)], x_fades)
+
+    def x_copy(bit, o):
+        block = lev.at[first_x + bit, c, y]
+        return copy(block, block, x_sem, bit * ny + o, lax.rem(y + o, ny) * 2 + c, wide)
+
     for bit in range(bx):
-        value = pick(found[bit], x // 2 ** (bit + 1))
-        lev[first_x + bit, c, y] = jnp.where(has(x, bit), value, 0.0)
-
-    def x_copy(o):
-        block = lev.at[pl.ds(first_x, bx), c, y]
-        return copy(block, block, x_sem, o, lax.rem(y + o, ny) * 2 + c, wide)
-
-    for o in range(1, ny):
-        x_copy(o).start()
+
+        @pl.when(has(x, bit))
+        def _():
+            lev[first_x + bit, c, y] = pick(found[bit], x // 2 ** (bit + 1))
+            for o in range(1, ny):
+                x_copy(bit, o).start()
+
+        @pl.when(jnp.logical_not(has(x, bit)))
+        def _():
+            lev[first_x + bit] = jnp.zeros(lev.shape[1:], F32)
 
     def forward(first, count, index):
         block = lev.at[pl.ds(first, count), c]
@@ -318,30 +339,52 @@
                 copy(block, block, y_sem, bit * ny + o, n, wide).wait_recv()
             forward(1 + bit, 1, bit).start()
 
-    hz[z] = hbuf[...]
+    def z_block(count, from_y, from_x):
+        rows = pl.ds(pl.multiple_of(from_x * part, part), part)
+        return lev.at[pl.ds(first_z, count), c, from_y, rows]
+
+    def z_copy(count, ox, oy):
+        return copy(
+            lvz.at[pl.ds(0, count)], z_block(count, y, x), z_sem, ox * ny + oy,
+            lax.rem(y + oy, ny) * 2 + c, z * nx + lax.rem(x + ox, nx),
+        )
+
+    def z_forward(count, parity, ox):
+        rows = pl.ds(pl.multiple_of(lax.rem(x + nx - ox, nx) * part, part), part)
+        block = lev.at[pl.ds(first_z, count), parity, :, rows]
+        return copy(block, block, f_sem, by + bx + ox, mate, wide)
+
+    others = [(ox, oy) for ox in range(nx) for oy in range(ny) if ox or oy]
+    near = sorted(range(nx), key=lambda o: min(o, nx - o))
+    slot_of = [sum([lax.rem(z // 2**i, 2) for i in range(bit)], z * 0) for bit in range(bz)]
+    held = sum([lax.rem(z // 2**i, 2) for i in range(bz)], z * 0)
     for o in range(1, nz):
-        source = lax.rem(z + nz - o, nz)
-        copy(hz.at[source], hz.at[source], p3_sem, o, n, wide).wait_recv()
+
+        @pl.when(z >= o)
+        def _():
+            copy(hz.at[z - o], hz.at[z - o], p3_sem, o, n, wide).wait_recv()
+
     z_totals = [hz[i, part:] for i in range(nz)]
     found, _ = tree([hz[i, :part] for i in range(nz)], [jnp.exp(hz[i, pl.ds(part + n, 1)]) for i in range(nz)])
     for bit in range(bz):
-        value = pick(found[bit], z // 2 ** (bit + 1))
-        lvz[bit] = jnp.where(has(z, bit), value, 0.0)
-
-    def z_block(from_y, from_x):
-        return lev.at[pl.ds(first_z, bz), c, from_y, pl.ds(pl.multiple_of(from_x * part, part), part)]
-
-    def z_copy(ox, oy):
-        return copy(
-            lvz, z_block(y, x), z_sem, ox * ny + oy,
-            lax.rem(y + oy, ny) * 2 + c, z * nx + lax.rem(x + ox, nx),
-        )
-
-    others = [(ox, oy) for ox in range(nx) for oy in range(ny) if ox or oy]
-    for ox, oy in others:
-        z_copy(ox, oy).start()
-    for bit in range(bz):
-        lev[first_z + bit, c, y, own_rows] = lvz[bit]
+
+        @pl.when(has(z, bit))
+        def _():
+            lvz[slot_of[bit]] = pick(found[bit], z // 2 ** (bit + 1))
+
+    for count in range(1, bz + 1):
+
+        @pl.when(held == count)
+        def _():
+            for ox, oy in others:
+                z_copy(count, ox, oy).start()
+            lev[first_z : first_z + count, c, y, own_rows] = lvz[:count]
+
+    for slot in range(bz):
+
+        @pl.when(held <= slot)
+        def _():
+            lev[first_z + slot] = jnp.zeros(lev.shape[1:], F32)
 
     def local_levels(h, carry):
         one = pl.ds(h, 1)
@@ -360,13 +403,6 @@
             acc_ref[h, :, here] += jnp.dot(left, right, preferred_element_type=F32)
         return carry
 
-    lax.fori_loop(0, heads, local_levels, 0)
-
-    for o in range(1, ny):
-        block = lev.at[pl.ds(first_x, bx), c, lax.rem(y + ny - o, ny)]
-        copy(block, block, x_sem, o, n, wide).wait_recv()
-    forward(first_x, bx, by).start()
-
     low = jnp.where(c == 1, mate_total, 0.0)
     chip_pre, y_running = prefixes(chip_totals, y)
     middle, x_running = prefixes(x_totals, x)
@@ -374,12 +410,43 @@
     base = low + y_running
     pres = [jnp.zeros_like(low)] + [low + v for v in chip_pre]
     pres += [base + v for v in middle] + [base + x_running + v for v in high]
-    for level, pre in enumerate(pres):
-        pre_ref[level] = pre[:heads]
+
+    def scale(level):
+        wide_pre = jnp.concatenate([pres[level][:heads]] * chunks, axis=1)
+        return w_ref[1 + local + level] * jnp.exp(cum_ref[...] + wide_pre)
+
     for level in range(first_z):
-        wide_pre = jnp.concatenate([pres[level][:heads]] * chunks, axis=1)
-        u_s[1 + local + level] = w_ref[1 + local + level] * jnp.exp(cum_ref[...] + wide_pre)
-
+        u_s[1 + local + level] = scale(level)
+    for bit in range(bz):
+        u_s[1 + local + first_z + bit] = jnp.zeros((heads, tokens), F32)
+    for bit in range(bz):
+
+        @pl.when(has(z, bit))
+        def _():
+            u_s[1 + local + first_z + slot_of[bit]] = scale(first_z + bit)
+
+    def z_rights(h, carry):
+        one = pl.ds(h, 1)
+        for slot in range(bz):
+            row = u_s[1 + local + first_z + slot, one, :]
+            right_ref[h, slot * 128 : (slot + 1) * 128, :] = (qt_ref[...] * row).astype(BF16)
+        return carry
+
+    def level_products(levels):
+        def body(h, carry):
+            one = pl.ds(h, 1)
+            left = jnp.concatenate([lev[level, lax.rem(h, 2), h // 2].astype(BF16) for level in levels], axis=1)
+            scales = [u_s[1 + local + level, one, :] for level in levels]
+            for i in range(spans):
+                here = slice(i * SPAN, (i + 1) * SPAN)
+                right = jnp.concatenate([(qt_ref[:, here] * row[:, here]).astype(BF16) for row in scales], axis=0)
+                acc_ref[h, :, here] += jnp.dot(left, right, preferred_element_type=F32)
+            return carry
+
+        lax.fori_loop(0, heads, body, 0)
+
+    lax.fori_loop(0, heads, z_rights, 0)
+    lax.fori_loop(0, heads, local_levels, 0)
     for bit in range(by):
 
         @pl.when(has(y, bit))
@@ -390,28 +457,35 @@
     def _():
         level0.wait_recv()
 
-    forwarded(first_x, bx, by).wait_recv()
-
-    def outer_levels(h, carry):
-        one = pl.ds(h, 1)
-        left = jnp.concatenate(
-            [lev[level, lax.rem(h, 2), h // 2].astype(BF16) for level in range(first_z)], axis=1
-        )
-        scales = [u_s[1 + local + level, one, :] for level in range(first_z)]
-        for i in range(spans):
-            here = slice(i * SPAN, (i + 1) * SPAN)
-            right = jnp.concatenate(
-                [(qt_ref[:, here] * scales[level][:, here]).astype(BF16) for level in range(first_z)], axis=0
-            )
-            acc_ref[h, :, here] += jnp.dot(left, right, preferred_element_type=F32)
-        return carry
-
-    lax.fori_loop(0, heads, outer_levels, 0)
-
-    for ox, oy in others:
-        block = z_block(lax.rem(y + ny - oy, ny), lax.rem(x + nx - ox, nx))
-        copy(block, block, z_sem, ox * ny + oy, n, wide).wait_recv()
-    forward(first_z, bz, by + 1).start()
+    level_products(range(first_x))
+
+    for bit in range(bx):
+
+        @pl.when(has(x, bit))
+        def _():
+            for o in range(1, ny):
+                block = lev.at[first_x + bit, c, lax.rem(y + ny - o, ny)]
+                copy(block, block, x_sem, bit * ny + o, n, wide).wait_recv()
+            forward(first_x + bit, 1, by + bit).start()
+
+    for count in range(1, bz + 1):
+
+        @pl.when(held == count)
+        def _():
+            for ox in near:
+                for oy in range(ny):
+                    if ox or oy:
+                        block = z_block(count, lax.rem(y + ny - oy, ny), lax.rem(x + nx - ox, nx))
+                        copy(block, block, z_sem, ox * ny + oy, n, wide).wait_recv()
+                z_forward(count, c, ox).start()
+
+    for bit in range(bx):
+
+        @pl.when(has(x, bit))
+        def _():
+            forwarded(first_x + bit, 1, by + bit).wait_recv()
+
+    level_products(range(first_x, first_z))
 
     swap.wait_send()
 
@@ -421,14 +495,23 @@
 
     for o in range(1, ny):
         p1(o).wait_send()
-        x_copy(o).wait_send()
     for o in range(1, nx):
         p2(o).wait_send()
         whole_x(o).wait_send()
     for o in range(1, nz):
-        p3(o).wait_send()
-    for ox, oy in others:
-        z_copy(ox, oy).wait_send()
+
+        @pl.when(z + o < nz)
+        def _():
+            p3(o).wait_send()
+
+    for bit in range(bx):
+
+        @pl.when(has(x, bit))
+        def _():
+            for o in range(1, ny):
+                x_copy(bit, o).wait_send()
+            forward(first_x + bit, 1, by + bit).wait_send()
+
     for bit in range(by):
         for o in range(1, ny):
 
@@ -440,15 +523,23 @@
         def _():
             forward(1 + bit, 1, bit).wait_send()
 
-    forward(first_x, bx, by).wait_send()
-    forwarded(first_z, bz, by + 1).wait_recv()
-    for level in range(bz):
+    for count in range(1, bz + 1):
+
+        @pl.when(held == count)
+        def _():
+            for ox, oy in others:
+                z_copy(count, ox, oy).wait_send()
+            for ox in near:
+                z_forward(count, 1 - c, ox).wait_recv()
+            for ox in near:
+                z_forward(count, c, ox).wait_send()
+
+    for slot in range(bz):
         for h in range(heads):
-            lev_ref[h, :, level * 128 : (level + 1) * 128] = lev[first_z + level, h % 2, h // 2].astype(BF16)
-    forward(first_z, bz, by + 1).wait_send()
-
-
-def main_part(ny, nx, nz, queries, keys, values, log_decay, level_weight):
+            lev_ref[h, :, slot * 128 : (slot + 1) * 128] = lev[first_z + slot, h % 2, h // 2].astype(BF16)
+
+
+def main_part(ny, nx, nz, queries, keys, values, log_decay, level_weight, gain):
     heads, tokens = log_decay.shape
     by, bx, bz = bits_of(ny), bits_of(nx), bits_of(nz)
     levels = 1 + by + bx + bz
@@ -460,12 +551,11 @@
         out_shape=(
             jax.ShapeDtypeStruct((heads, 128, tokens), F32),
             jax.ShapeDtypeStruct((heads, 128, bz * 128), BF16),
-            jax.ShapeDtypeStruct((levels, heads, 128), F32),
-            jax.ShapeDtypeStruct((heads, tokens), F32),
-            jax.ShapeDtypeStruct((128, tokens), F32),
+            jax.ShapeDtypeStruct((heads, bz * 128, tokens), BF16),
+            jax.ShapeDtypeStruct(gain.shape, F32),
         ),
-        in_specs=[pl.BlockSpec(memory_space=pltpu.HBM)] * 5,
-        out_specs=(VMEM,) * 5,
+        in_specs=[pl.BlockSpec(memory_space=pltpu.HBM)] * 6,
+        out_specs=(VMEM,) * 4,
         scratch_shapes=[
             pltpu.VMEM((2, ny, 136, 128), F32),
             pltpu.VMEM((ny, 136, 128), F32),
@@ -484,7 +574,10 @@
             pltpu.VMEM((spans, heads, 128, 128), F32),
             pltpu.VMEM((spans, heads, 128, 128), F32),
             pltpu.VMEM((4, heads, tokens), F32),
-            pltpu.VMEM((1 + bits_of(spans) + 1 + by + bx, heads, tokens), F32),
+            pltpu.VMEM((1 + bits_of(spans) + levels, heads, tokens), F32),
+            pltpu.VMEM((heads, tokens), F32),
+            pltpu.VMEM((128, tokens), F32),
+            pltpu.VMEM((heads, tokens), F32),
             dma((2, 1)),
             dma((2, 1)),
             dma((2, ny)),
@@ -492,10 +585,10 @@
             dma((2, nx)),
             dma((2, nz)),
             dma((2, by * ny)),
-            dma((2, ny)),
+            dma((2, bx * ny)),
             dma((2, nx * ny)),
-            dma((2, by + 2)),
-            dma((5,)),
+            dma((2, by + bx + nx)),
+            dma((6,)),
             pltpu.VMEM(queries.shape, queries.dtype),
             pltpu.VMEM(keys.shape, keys.dtype),
             pltpu.VMEM(values.shape, values.dtype),
@@ -503,48 +596,46 @@
             pltpu.VMEM(level_weight.shape, level_weight.dtype),
         ],
         compiler_params=pltpu.CompilerParams(collective_id=0, has_side_effects=True, vmem_limit_bytes=40 * 2**20),
-    )(*[pltpu.with_memory_space_constraint(v, pltpu.HBM) for v in (queries, keys, values, log_decay, level_weight)])
-
-
-def finish_kernel(skip, qt_ref, lev_ref, pre_ref, cum_ref, w_ref, acc_ref, gain_ref, out_ref):
-    heads, tokens = cum_ref.shape
-    levels = lev_ref.shape[2] // 128
-    first = w_ref.shape[0] - levels
+    )(*[pltpu.with_memory_space_constraint(v, pltpu.HBM) for v in (queries, keys, values, log_decay, level_weight, gain)])
+
+
+def finish_kernel(acc_ref, lev_ref, right_ref, gain_ref, out_hbm, out_s, sems):
+    heads, _, tokens = acc_ref.shape
     gain = gain_ref[...]
-    for h in range(heads):
-        for i in range(tokens // SPAN):
-            at = slice(i * SPAN, (i + 1) * SPAN)
-            qt = qt_ref[:, at]
-            cum = cum_ref[h : h + 1, at]
-            right = []
-            for level in range(levels):
-                pre = pre_ref[skip + level, h : h + 1, :]
-                pre = jnp.concatenate([pre, pre], axis=1)
-                right.append((qt * (w_ref[first + level, h : h + 1, at] * jnp.exp(cum + pre))).astype(BF16))
-            mixed = acc_ref[h, :, at] + jnp.dot(
-                lev_ref[h], jnp.concatenate(right, axis=0), preferred_element_type=F32
-            )
+    sends = []
+    for i in range(tokens // SPAN):
+        at = slice(i * SPAN, (i + 1) * SPAN)
+        for h in range(heads):
+            mixed = acc_ref[h, :, at] + jnp.dot(lev_ref[h], right_ref[h, :, at], preferred_element_type=F32)
             square = jnp.mean(mixed * mixed, axis=0, keepdims=True)
             normed = (mixed * lax.rsqrt(square + 1e-05)).T
-            out_ref[at, h * 128 : (h + 1) * 128] = (normed * gain[:, h * 128 : (h + 1) * 128]).astype(BF16)
-
-
-def finish_part(skip, qt, lev, pre, cum, level_weight, acc, gain):
-    heads, tokens = cum.shape
+            out_s[at, h * 128 : (h + 1) * 128] = (normed * gain[:, h * 128 : (h + 1) * 128]).astype(BF16)
+        send = pltpu.make_async_copy(out_s.at[at], out_hbm.at[at], sems.at[i])
+        send.start()
+        sends.append(send)
+    for send in sends:
+        send.wait()
+
+
+def finish_part(acc, lev, right, gain):
+    heads, _, tokens = acc.shape
     return pl.pallas_call(
-        functools.partial(finish_kernel, skip),
+        finish_kernel,
         out_shape=jax.ShapeDtypeStruct((tokens, heads * 128), BF16),
-        in_specs=[VMEM] * 7,
-        out_specs=VMEM,
+        in_specs=[VMEM] * 4,
+        out_specs=pl.BlockSpec(memory_space=pl.ANY),
+        scratch_shapes=[
+            pltpu.VMEM((tokens, heads * 128), BF16),
+            pltpu.SemaphoreType.DMA((tokens // SPAN,)),
+        ],
         compiler_params=pltpu.CompilerParams(vmem_limit_bytes=24 * 2**20),
-    )(qt, lev, pre, cum, level_weight, acc, gain)
+    )(acc, lev, right, gain)
 
 
 def per_device(sizes, queries, keys, values, log_decay, level_weight, norm_gain):
     ny, nx, nz = sizes
-    acc, lev, pre, cum, qt = main_part(ny, nx, nz, queries, keys, values, log_decay, level_weight)
-    skip = pre.shape[0] - lev.shape[2] // 128
-    return finish_part(skip, qt, lev, pre, cum, level_weight, acc, norm_gain.reshape(1, -1))
+    gain = norm_gain.reshape(1, -1)
+    return finish_part(*main_part(ny, nx, nz, queries, keys, values, log_decay, level_weight, gain))
 
 
 def solution(mesh, nx=4):

time: 51.3 us -> 40.8 us (0.80)
  the two profiles are of different devices: /device:TPU:1 before, /device:TPU:230 now
where the time goes in v3:
time: 40.8 us; the launch traced here: 40.3 us
  Pallas kernels  40.2 us (99%)
    pallas_call x1, Pallas kernels, main_part(): pl.pallas_call(functools.partial(main_kernel, ny, nx, nz), out_shape=(jax...  37.7 us
    pallas_call x1, Pallas kernels, finish_part(): pl.pallas_call(finish_kernel, out_shape=jax.ShapeDtypeStruct((tokens, hea...  2.56 us

profile of v3, /device:TPU:230, one launch (start us, length us, event | category | flops | bytes accessed | tf_op | source)
XLA Modules:
  0.0 40.3 jit_solution(9481454064231125313)
XLA Ops:
  0.0 37.7 %shard_map.64 = (f32[8,128,1024]{2,1,0:T(8,128)S(1)}, bf16[8,128,384]{2,1,0:T(8,128)(2,1)S(1)}, bf16[8,384,1024]{2,1,0:T(8,128)(2,1)S(1)}, f32[1,1024]{1,0:T(1,128)S(1)}) custom-call(bf16[1024,128]{1,0:T(8,128)(2,1)} %q_hbm.1, bf16[1024,128]{1,0:T(8,128)(2,1)} %k_hbm.1, bf16[1024,1024]{1,0:T(8,128)(2,1)} %v_hbm.1, f32[8,1024]{1,0:T(8,128)} %d_hbm.1, ...), custom_call_target="tpu_custom_call" | custom-call | tf_op jit(solution)/shard_map/pallas_call | solution.py:549
  37.7 2.6 %shard_map.65 = bf16[1024,1024]{1,0:T(8,128)(2,1)} custom-call(f32[8,128,1024]{2,1,0:T(8,128)S(1)} %get-tuple-element.9.acc_ref, bf16[8,128,384]{2,1,0:T(8,128)(2,1)S(1)} %get-tuple-element.10.lev_ref, bf16[8,384,1024]{2,1,0:T(8,128)(2,1)S(1)} %get-tuple-element.11.right_ref, f32[1,1024]{1,0:T(1,128)S(1)} %get-tuple-element.12.gain_ref), custom_call_target="tpu_custom_call" | custom-call | tf_op jit(solution)/shard_map/pallas_call | solution.py:622

commit v4 on v3

--- a/solution.py
+++ b/solution.py
@@ -21,6 +21,10 @@
 
 def columns(index, width):
     return pl.ds(pl.multiple_of(index * width, width), width)
+
+
+def far_first(n):
+    return sorted(range(1, n), key=lambda o: -min(o, n - o))
 
 
 def bits_of(n):
@@ -102,24 +106,22 @@
         fetch.start()
 
     barrier = pltpu.get_barrier_semaphore()
-    peers = 0
 
     def hello(to_n, to_wide):
         pl.semaphore_signal(barrier, inc=1, device_id={"narrow": to_n, "wide": to_wide}, device_id_type=MESH)
 
-    for o in range(1, nz):
+    others = [(ox, oy) for ox in range(nx) for oy in range(ny) if ox or oy]
+    others.sort(key=lambda o: -min(o[0], nx - o[0]) - min(o[1], ny - o[1]))
+    for ox, oy in others:
+        hello(lax.rem(y + oy, ny) * 2 + c, z * nx + lax.rem(x + ox, nx))
+    for o in far_first(nz):
 
         @pl.when(z >= o)
         def _():
             hello(n, (z - o) * nx + x)
 
-    for ox in range(nx):
-        for oy in range(ny):
-            if ox or oy:
-                hello(lax.rem(y + oy, ny) * 2 + c, z * nx + lax.rem(x + ox, nx))
-                peers += 1
     hello(mate, wide)
-    peers += 1
+    peers = len(others) + 1
 
     fetches[0].wait()
     at = [slice(m * CHUNK, (m + 1) * CHUNK) for m in range(chunks)]
@@ -183,7 +185,7 @@
         to = lax.rem(y + o, ny)
         return copy(chip_buf.at[to], r1.at[y], p1_sem, o, to * 2 + c, wide)
 
-    for o in range(1, ny):
+    for o in far_first(ny):
         p1(o).start()
 
     fetches[3].wait()
@@ -241,13 +243,22 @@
         to = lax.rem(x + o, nx)
         return copy(gq.at[to], gxq.at[x], p2_sem, o, n, z * nx + to)
 
-    def whole_x(o):
-        return copy(gbuf, gx.at[x], g_sem, o, n, z * nx + lax.rem(x + o, nx))
-
-    for o in range(1, nx):
+    def x_send(bit, src, oy, to_x):
+        return copy(
+            src, lev.at[first_x + bit, c, y], x_sem, bit * ny + oy,
+            lax.rem(y + oy, ny) * 2 + c, z * nx + to_x,
+        )
+
+    def x_arrived(bit, oy):
+        block = lev.at[first_x + bit, c, lax.rem(y + ny - oy, ny)]
+        copy(block, block, x_sem, bit * ny + oy, n, wide).wait_recv()
+
+    def to_row_before():
+        return copy(gbuf, gx.at[0], g_sem, 0, n, wide - 1)
+
+    for o in far_first(nx):
         p2(o).start()
-    for o in range(1, nx):
-        whole_x(o).start()
+
     slot = 0
     slots = []
     for bit in range(by):
@@ -278,7 +289,6 @@
             lev[1 + bit] = jnp.zeros(lev.shape[1:], F32)
 
     gxq[x] = gq[x]
-    gx[x] = gbuf[...]
     for o in range(1, nx):
         source = lax.rem(x + nx - o, nx)
         copy(gxq.at[source], gxq.at[source], p2_sem, o, n, wide).wait_recv()
@@ -294,32 +304,46 @@
     def p3(o):
         return copy(hbuf, hz.at[z], p3_sem, o, n, (z + o) * nx + x)
 
-    for o in range(1, nz):
+    for o in far_first(nz):
 
         @pl.when(z + o < nz)
         def _():
             p3(o).start()
 
-    for o in range(1, nx):
-        source = lax.rem(x + nx - o, nx)
-        copy(gx.at[source], gx.at[source], g_sem, o, n, wide).wait_recv()
-    found, _ = tree([gx[i] for i in range(nx)], x_fades)
-
-    def x_copy(bit, o):
-        block = lev.at[first_x + bit, c, y]
-        return copy(block, block, x_sem, bit * ny + o, lax.rem(y + o, ny) * 2 + c, wide)
-
-    for bit in range(bx):
-
-        @pl.when(has(x, bit))
-        def _():
-            lev[first_x + bit, c, y] = pick(found[bit], x // 2 ** (bit + 1))
-            for o in range(1, ny):
-                x_copy(bit, o).start()
-
-        @pl.when(jnp.logical_not(has(x, bit)))
-        def _():
-            lev[first_x + bit] = jnp.zeros(lev.shape[1:], F32)
+    if bx > 1:
+
+        @pl.when(x == 1)
+        def _():
+            to_row_before().start()
+
+    @pl.when(jnp.logical_not(has(x, 0)))
+    def _():
+        for oy in range(ny):
+            x_send(0, gbuf, oy, x + 1).start()
+        lev[first_x] = jnp.zeros(lev.shape[1:], F32)
+
+    @pl.when(has(x, 0))
+    def _():
+        x_arrived(0, 0)
+
+    if bx > 1:
+
+        @pl.when(x == 1)
+        def _():
+            gx[1] = lev[first_x, c, y] * x_fades[1] + gbuf[...]
+            for oy in range(ny):
+                x_send(1, gx.at[1], oy, 2).start()
+
+        @pl.when(x == 0)
+        def _():
+            copy(gx.at[0], gx.at[0], g_sem, 0, n, wide).wait_recv()
+            gx[1] = gbuf[...] * x_fades[1] + gx[0]
+            for oy in range(ny):
+                x_send(1, gx.at[1], oy, 3).start()
+
+        @pl.when(jnp.logical_not(has(x, 1)))
+        def _():
+            lev[first_x + 1] = jnp.zeros(lev.shape[1:], F32)
 
     def forward(first, count, index):
         block = lev.at[pl.ds(first, count), c]
@@ -354,7 +378,6 @@
         block = lev.at[pl.ds(first_z, count), parity, :, rows]
         return copy(block, block, f_sem, by + bx + ox, mate, wide)
 
-    others = [(ox, oy) for ox in range(nx) for oy in range(ny) if ox or oy]
     near = sorted(range(nx), key=lambda o: min(o, nx - o))
     slot_of = [sum([lax.rem(z // 2**i, 2) for i in range(bit)], z * 0) for bit in range(bz)]
     held = sum([lax.rem(z // 2**i, 2) for i in range(bz)], z * 0)
@@ -463,9 +486,8 @@
 
         @pl.when(has(x, bit))
         def _():
-            for o in range(1, ny):
-                block = lev.at[first_x + bit, c, lax.rem(y + ny - o, ny)]
-                copy(block, block, x_sem, bit * ny + o, n, wide).wait_recv()
+            for oy in range(1 if bit == 0 else 0, ny):
+                x_arrived(bit, oy)
             forward(first_x + bit, 1, by + bit).start()
 
     for count in range(1, bz + 1):
@@ -497,7 +519,6 @@
         p1(o).wait_send()
     for o in range(1, nx):
         p2(o).wait_send()
-        whole_x(o).wait_send()
     for o in range(1, nz):
 
         @pl.when(z + o < nz)
@@ -508,9 +529,25 @@
 
         @pl.when(has(x, bit))
         def _():
-            for o in range(1, ny):
-                x_copy(bit, o).wait_send()
             forward(first_x + bit, 1, by + bit).wait_send()
+
+    @pl.when(jnp.logical_not(has(x, 0)))
+    def _():
+        for oy in range(ny):
+            x_send(0, gbuf, oy, x + 1).wait_send()
+
+    if bx > 1:
+
+        @pl.when(x == 1)
+        def _():
+            to_row_before().wait_send()
+            for oy in range(ny):
+                x_send(1, gx.at[1], oy, 2).wait_send()
+
+        @pl.when(x == 0)
+        def _():
+            for oy in range(ny):
+                x_send(1, gx.at[1], oy, 3).wait_send()
 
     for bit in range(by):
         for o in range(1, ny):
@@ -564,7 +601,7 @@
             pltpu.VMEM((nx, part + 8, 128), F32),
             pltpu.VMEM((nx, part + 8, 128), F32),
             pltpu.VMEM((128, 128), F32),
-            pltpu.VMEM((nx, 128, 128), F32),
+            pltpu.VMEM((2, 128, 128), F32),
             pltpu.VMEM((part + 8, 128), F32),
             pltpu.VMEM((nz, part + 8, 128), F32),
             pltpu.VMEM((levels, 2, ny, 128, 128), F32),
@@ -582,7 +619,7 @@
             dma((2, 1)),
             dma((2, ny)),
             dma((2, nx)),
-            dma((2, nx)),
+            dma((2, 1)),
             dma((2, nz)),
             dma((2, by * ny)),
             dma((2, bx * ny)),

time: 40.8 us -> 39 us (0.956); the launches traced: 40.3 us -> 38.9 us
  Pallas kernels: 40.2 us -> 38.9 us
    pallas_call x1, Pallas kernels: 37.7 us -> 36.4 us  [main_part(): pl.pallas_call(functools.partial(main_kernel, ny, nx, nz), out_shape=(jax...]
where the time goes in v4:
time: 39 us; the launch traced here: 38.9 us
  Pallas kernels  38.9 us (100%)
    pallas_call x1, Pallas kernels, main_part(): pl.pallas_call(functools.partial(main_kernel, ny, nx, nz), out_shape=(jax...  36.4 us
    pallas_call x1, Pallas kernels, finish_part(): pl.pallas_call(finish_kernel, out_shape=jax.ShapeDtypeStruct((tokens, hea...  2.56 us

profile of v4, /device:TPU:230, one launch (start us, length us, event | category | flops | bytes accessed | tf_op | source)
XLA Modules:
  0.0 38.9 jit_solution(14879541086090423352)
XLA Ops:
  0.0 36.4 %shard_map.64 = (f32[8,128,1024]{2,1,0:T(8,128)S(1)}, bf16[8,128,384]{2,1,0:T(8,128)(2,1)S(1)}, bf16[8,384,1024]{2,1,0:T(8,128)(2,1)S(1)}, f32[1,1024]{1,0:T(1,128)S(1)}) custom-call(bf16[1024,128]{1,0:T(8,128)(2,1)} %q_hbm.1, bf16[1024,128]{1,0:T(8,128)(2,1)} %k_hbm.1, bf16[1024,1024]{1,0:T(8,128)(2,1)} %v_hbm.1, f32[8,1024]{1,0:T(8,128)} %d_hbm.1, ...), custom_call_target="tpu_custom_call" | custom-call | tf_op jit(solution)/shard_map/pallas_call | solution.py:586
  36.4 2.6 %shard_map.65 = bf16[1024,1024]{1,0:T(8,128)(2,1)} custom-call(f32[8,128,1024]{2,1,0:T(8,128)S(1)} %get-tuple-element.9.acc_ref, bf16[8,128,384]{2,1,0:T(8,128)(2,1)S(1)} %get-tuple-element.10.lev_ref, bf16[8,384,1024]{2,1,0:T(8,128)(2,1)S(1)} %get-tuple-element.11.right_ref, f32[1,1024]{1,0:T(1,128)S(1)} %get-tuple-element.12.gain_ref), custom_call_target="tpu_custom_call" | custom-call | tf_op jit(solution)/shard_map/pallas_call | solution.py:659

commit v5 on v4

--- a/solution.py
+++ b/solution.py
@@ -164,10 +164,6 @@
 
     @pl.when(c == 0)
     def _():
-        level0.start()
-
-    @pl.when(c == 0)
-    def _():
         lev[0] = jnp.zeros(lev.shape[1:], F32)
 
     swap.wait_recv()
@@ -187,6 +183,10 @@
 
     for o in far_first(ny):
         p1(o).start()
+
+    @pl.when(c == 0)
+    def _():
+        level0.start()
 
     fetches[3].wait()
     fetches[4].wait()

time: 39 us -> 39 us (level)
  no operation moved by 1% of the time
where the time goes in v5:
time: 39 us; the launch traced here: 38.9 us
  Pallas kernels  38.9 us (100%)
    pallas_call x1, Pallas kernels, main_part(): pl.pallas_call(functools.partial(main_kernel, ny, nx, nz), out_shape=(jax...  36.3 us
    pallas_call x1, Pallas kernels, finish_part(): pl.pallas_call(finish_kernel, out_shape=jax.ShapeDtypeStruct((tokens, hea...  2.56 us

profile of v5, /device:TPU:230, one launch (start us, length us, event | category | flops | bytes accessed | tf_op | source)
XLA Modules:
  0.0 38.9 jit_solution(11735262196217298393)
XLA Ops:
  0.0 36.3 %shard_map.64 = (f32[8,128,1024]{2,1,0:T(8,128)S(1)}, bf16[8,128,384]{2,1,0:T(8,128)(2,1)S(1)}, bf16[8,384,1024]{2,1,0:T(8,128)(2,1)S(1)}, f32[1,1024]{1,0:T(1,128)S(1)}) custom-call(bf16[1024,128]{1,0:T(8,128)(2,1)} %q_hbm.1, bf16[1024,128]{1,0:T(8,128)(2,1)} %k_hbm.1, bf16[1024,1024]{1,0:T(8,128)(2,1)} %v_hbm.1, f32[8,1024]{1,0:T(8,128)} %d_hbm.1, ...), custom_call_target="tpu_custom_call" | custom-call | tf_op jit(solution)/shard_map/pallas_call | solution.py:586
  36.3 2.6 %shard_map.65 = bf16[1024,1024]{1,0:T(8,128)(2,1)} custom-call(f32[8,128,1024]{2,1,0:T(8,128)S(1)} %get-tuple-element.9.acc_ref, bf16[8,128,384]{2,1,0:T(8,128)(2,1)S(1)} %get-tuple-element.10.lev_ref, bf16[8,384,1024]{2,1,0:T(8,128)(2,1)S(1)} %get-tuple-element.11.right_ref, f32[1,1024]{1,0:T(1,128)S(1)} %get-tuple-element.12.gain_ref), custom_call_target="tpu_custom_call" | custom-call | tf_op jit(solution)/shard_map/pallas_call | solution.py:659
